TPU v7x, 128 devices: a whole 4x4x4 slice. The times are simulated.
128 devices in a mesh: ex: 8 (over y, x_hi), pb: 16 (over z, x_lo, core).
Axes of the slice: x: 4 (x_hi: 2, x_lo: 2; x = x_hi * 2 + x_lo), y: 4, z: 4, core: 2. Of those that a mesh axis runs over, the one named last changes fastest.
Arguments:
- train_features: bfloat16 [131072, 4096], P('ex', 'pb'), may hold values from -6 to 6
- query_features: bfloat16 [2048, 4096], P('ex', 'pb'), may hold values from -6 to 6
- precond: bfloat16 [4096, 4096], P('pb'), may hold values from -0.09375 to 0.09375
- example_weight: float32 [131072], P(('ex', 'pb')), may hold values from 0.05 to 0.95
- select: int32 [16, 1024], P(None, ('ex', 'pb')), may hold values from 0 to 1, as said below
Outputs:
- scores: float32 [2048, 131072], P(None, ('ex', 'pb'))
Inputs may be any that keep to these rules, and one draw needn't show every extreme that they name: `select`: 1 where the pair of query block and training block is to be scored, else 0; the number of listed pairs differs widely between query blocks and between training blocks.
All inputs are finite; a program needn't handle non-finite values.
Results may differ from a plain program's by a relative error of at most 0.0029.
Values may be sent and summed in bfloat16 or wider, within the bound.
No kernel may reach another device: no remote copies, remote signals or barrier semaphores. Data moves between devices by JAX's collectives and lax.ppermute only.
A program may use at most 128 MiB of HBM per device.

v0:
```python
import jax
import jax.numpy as jnp
from jax import lax
from jax.sharding import PartitionSpec as P

BLK = 128


def tile_product(portion, train_tile):
    return lax.dot_general(
        portion, train_tile, (((1,), (1,)), ((), ())), preferred_element_type=jnp.float32
    )


def on_device(train_features, query_features, precond, example_weight, select):
    rows_here = lax.all_to_all(train_features, "pb", split_axis=0, concat_axis=1, tiled=True)
    feature_width = rows_here.shape[1]
    gathered = lax.psum(
        jnp.dot(query_features, precond, preferred_element_type=jnp.float32), "pb"
    ).astype(jnp.bfloat16)
    block_count = select.shape[0]
    train_blocks = select.shape[1]
    product_part = tile_product(lax.all_gather(gathered, "ex", axis=0, tiled=True), rows_here)
    scaled = product_part * feature_width ** (-0.5) * example_weight[None, :]
    keep_mask = select.astype(jnp.float32)
    masked = scaled.reshape(block_count, BLK, train_blocks, BLK) * keep_mask[:, None, :, None]
    return masked.reshape(product_part.shape)


def solution(mesh):
    placed = (P("ex", "pb"), P("ex", "pb"), P("pb", None), P(("ex", "pb")), P(None, ("ex", "pb")))
    return jax.shard_map(
        on_device, mesh=mesh, in_specs=placed, out_specs=P(None, ("ex", "pb")), check_vma=False
    )
```

profile of v0, /device:TPU:1, one launch (start us, length us, event | category | flops | bytes accessed | tf_op | source)
XLA Modules:
  0.0 383.1 jit_solution(517960048451074875)
XLA Ops:
  6.5 0.0 copy-start
  6.5 0.0 all-gather.2.cloned.1.call-start
  6.5 1.6 copy-done
  8.1 3.6 fusion
  11.8 97.5 %all-reduce.1 = bf16[256,4096]{1,0:T(8,128)(2,1)} all-reduce(f32[256,4096]{1,0:T(8,128)} %fusion), channel_id=1, replica_groups=mesh['ex'=8,'pb'=16] {'pb'}, use_global_device_ids=true, to_apply=%region_0.0 | all-reduce | flops 1048576 | bytes 6291456 | tf_op jit(solution)/shard_map/psum | solution.py:18
  109.3 0.0 all-gather.2.cloned.1.call-update
  109.3 0.0 copy-start.3
  109.3 0.0 copy-start.4
  109.3 7.5 %all-to-all-start = ((bf16[16,1024,256]{2,1,0:T(8,128)(2,1)}), bf16[16,1024,256]{2,1,0:T(8,128)(2,1)}, u32[]{:S(2)}, u32[]{:S(2)}) async-start(bf16[16,1024,256]{2,1,0:T(8,128)(2,1)} %bitcast.12), calls=%async_computation | async-start | bytes 16777216 | tf_op jit(solution)/shard_map/all_to_all | solution.py:16
  116.8 0.0 copy-done.3
  116.8 0.1 copy.9
  116.9 0.0 copy-done.4
  116.9 150.3 %all-to-all-done = bf16[16,1024,256]{2,1,0:T(8,128)(2,1)} async-done(((bf16[16,1024,256]{2,1,0:T(8,128)(2,1)}), bf16[16,1024,256]{2,1,0:T(8,128)(2,1)}, u32[]{:S(2)}, u32[]{:S(2)}) %all-to-all-start) | async-done | bytes 8388640 | tf_op jit(solution)/shard_map/all_to_all | solution.py:16
  267.2 12.2 %copy.8 = bf16[1024,16,256]{0,2,1:T(8,128)(2,1)} copy(bf16[1024,16,256]{2,0,1:T(8,128)(2,1)} %bitcast.1) | data formatting | bytes 16777216 | tf_op jit(solution)/shard_map/all_to_all | solution.py:16
  279.5 70.8 %all-gather.2.cloned.1.call-done = bf16[2048,4096]{1,0:T(8,128)(2,1)} async-done(((bf16[256,4096]{1,0:T(8,128)(2,1)}), bf16[2048,4096]{1,0:T(8,128)(2,1)}) %all-gather.2.cloned.1.call-update) | async-done | bytes 16777232 | tf_op jit(solution)/shard_map/all_gather | solution.py:23
  350.3 0.0 copy-start.2
  350.3 0.6 mul.29
  350.9 2.8 copy-done.2
  353.7 0.0 copy-start.1
  353.7 22.6 %bitcast_multiply_fusion = f32[2048,1024]{1,0:T(8,128)} fusion(f32[256,8,8,128]{3,2,1,0:T(8,128)S(1)} %bitcast.11, bf16[2048,4096]{1,0:T(8,128)(2,1)} %all-gather.2.cloned.1.call-done, bf16[1024,4096]{0,1:T(8,128)(2,1)S(1)} %bitcast.13, f32[1024]{0:T(1024)S(1)} %broadcast_multiply_fusion), kind=kOutput, calls=%fused_computation | convolution fusion | flops 17184063488 | bytes 41947136 | tf_op jit(solution)/shard_map/dot_general | solution.py:10
  376.3 0.0 copy-done.1
  (2 shorter events, 0.0 us)
Async XLA Ops:
  6.5 1.6 copy-start
  6.5 343.8 %all-gather.2.cloned.1.call-start = ((), (), s32[]{:S(2)}) async-start(), calls=%async_computation.1 | async-start | bytes 18874368 | tf_op jit(solution)/shard_map/all_gather | solution.py:23
  109.3 7.5 %copy-start.3 = (s32[16,8]{0,1:T(8,128)S(1)}, s32[16,8]{0,1:T(8,128)}, u32[]{:S(2)}) copy-start(s32[16,8]{0,1:T(8,128)} %param.9) | copy-start | bytes 1540
  109.3 7.6 %copy-start.4 = (f32[1024]{0:T(1024)S(1)}, f32[1024]{0:T(1024)}, u32[]{:S(2)}) copy-start(f32[1024]{0:T(1024)} %param.8) | copy-start | bytes 12292
  109.3 157.9 %all-to-all-start = ((bf16[16,1024,256]{2,1,0:T(8,128)(2,1)}), bf16[16,1024,256]{2,1,0:T(8,128)(2,1)}, u32[]{:S(2)}, u32[]{:S(2)}) async-start(bf16[16,1024,256]{2,1,0:T(8,128)(2,1)} %bitcast.12), calls=%async_computation | async-start | bytes 16777216 | tf_op jit(solution)/shard_map/all_to_all | solution.py:16
  350.3 3.4 copy-start.2
  353.7 22.6 %copy-start.1 = (bf16[256,4096]{1,0:T(8,128)(2,1)S(1)}, bf16[256,4096]{1,0:T(8,128)(2,1)}, u32[]{:S(2)}) copy-start(bf16[256,4096]{1,0:T(8,128)(2,1)} %param.7) | copy-start | bytes 6291460
Sparse Core Ops, SparseCore 0:
  109.4 240.8 all-gather.1
where the time goes:
time: 384 us; the launch traced here: 383 us
  waiting for transfers between devices  221 us (58%)
  blocking collectives  97.5 us (25%)
  matrix products  26.2 us (7%)
  local copies, waits for them, and re-layouts  17.3 us (5%)
  between operations  13.4 us (3%)
  starting transfers between devices  7.52 us (2%)
    all_to_all x1, waiting for transfers between devices, on_device(): lax.all_to_all(train_features, 'pb', split_axis=0, concat_axis=1, tiled=T...  150 us
    psum x1, blocking collectives, on_device(): lax.psum(jnp.dot(query_features, precond, preferred_element_type=jnp.floa...  97.5 us
    all_gather x1, waiting for transfers between devices, on_device(): lax.all_gather(gathered, 'ex', axis=0, tiled=True)  70.8 us
    dot_general x1, matrix products, tile_product(): lax.dot_general(portion, train_tile, (((1,), (1,)), ((), ())), preferred_...  22.6 us
    all_to_all x1, local copies, waits for them, and re-layouts, on_device(): lax.all_to_all(train_features, 'pb', split_axis=0, concat_axis=1, tiled=T...  12.2 us
  transfers between devices with their start and end apart: 2, of which 2 were waited for; matrix products, arithmetic and copies ran while one was open for 3% of the time, Pallas kernels for 0%

commit v1 on v0

v1 whole, which is shorter than its diff:
```python
import jax
import jax.numpy as jnp
from jax import lax
from jax.experimental import pallas as pl
from jax.experimental.pallas import tpu as pltpu
from jax.sharding import Mesh, PartitionSpec as P

BLK = 128
PB = ("z", "xl", "c")
PLANE = ("xh", "z", "xl")
WIDTHS = (768, 256)

IN_VMEM = pl.BlockSpec(memory_space=pltpu.VMEM)
IN_SMEM = pl.BlockSpec(memory_space=pltpu.SMEM)


def shift(x, by):
    return lax.ppermute(x, "y", [(i, (i + by) % 4) for i in range(4)])


def swap(x):
    return lax.ppermute(x, "c", [(0, 1), (1, 0)])


def split_kernel(where, p, out):
    cols = out.shape[2]
    for j in range(out.shape[0]):
        out[j] = p[:, j * cols : (j + 1) * cols]


def split_quarter(where, precond, cols):
    rows = precond.shape[0] // 4
    blocks = precond.shape[1] // cols
    return pl.pallas_call(
        split_kernel,
        grid_spec=pltpu.PrefetchScalarGridSpec(
            num_scalar_prefetch=1,
            grid=(1,),
            in_specs=[pl.BlockSpec((rows, precond.shape[1]), lambda i, where: (where[0], 0))],
            out_specs=pl.BlockSpec((blocks, rows, cols), lambda i, where: (0, 0, 0)),
        ),
        out_shape=jax.ShapeDtypeStruct((blocks, rows, cols), precond.dtype),
        compiler_params=pltpu.CompilerParams(vmem_limit_bytes=8 * 2**20),
    )(where, precond)


def tile_kernel(where, p0, p1, p2, p3, own, other, out, whole):
    y, core = where[0], where[1]
    quarter = p0.shape[1]
    for back, piece in enumerate((p0, p1, p2, p3)):
        start = pl.multiple_of(lax.rem(y + 4 - back, 4) * quarter, quarter)
        whole[:, pl.ds(start, quarter), :] = piece[...]
    acc = None
    for s in range(8):
        for half, q in enumerate((own, other)):
            side = core if half == 0 else 1 - core
            part = jnp.dot(q[s], whole[2 * s + side], preferred_element_type=jnp.float32)
            acc = part if acc is None else acc + part
    tile = acc.astype(out.dtype)
    for s in range(out.shape[0]):
        out[s] = tile


def conditioned_tiles(where, pieces, own, other):
    rows = own.shape[1]
    return pl.pallas_call(
        tile_kernel,
        in_specs=[IN_SMEM] + [IN_VMEM] * 6,
        out_specs=IN_VMEM,
        out_shape=jax.ShapeDtypeStruct((16, rows, rows), jnp.bfloat16),
        scratch_shapes=[pltpu.VMEM((16, rows, rows), jnp.bfloat16)],
        compiler_params=pltpu.CompilerParams(vmem_limit_bytes=16 * 2**20),
    )(where, *pieces, own, other)


def score_kernel(n_units, where, *refs):
    units, (train, factor, out) = refs[: 2 * n_units], refs[2 * n_units :][-3:]
    core = where[1]
    for j in range(n_units):

        @pl.when(pl.program_id(0) == j)
        def _():
            acc = None
            for half in range(2):
                side = core if half == 0 else 1 - core
                for s in range(8):
                    part = lax.dot_general(
                        units[2 * j + half][s],
                        train[2 * s + side],
                        (((1,), (1,)), ((), ())),
                        preferred_element_type=jnp.float32,
                    )
                    acc = part if acc is None else acc + part
            rows = acc.shape[0] // 2
            out[:rows, :] = acc[:rows] * factor[0, 0:1, :]
            out[rows:, :] = acc[rows:] * factor[0, 1:2, :]


def scores(where, units, train, factor, column, total, previous):
    n = len(units)
    width, rows = train.shape[1], units[0][0].shape[1]

    def block_row(i, where):
        row = 0
        for j, (_, _, offset, xh) in enumerate(units):
            row = jnp.where(i == j, lax.rem(where[0] + offset, 4) * 2 + xh, row)
        return row

    operands = [x for unit in units for x in unit[:2]]
    in_specs = [IN_VMEM] * len(operands)
    aliases = {}
    if previous is not None:
        aliases = {1 + len(operands): 0}
        in_specs.append(pl.BlockSpec(memory_space=pl.ANY))
        operands.append(previous)
    in_specs += [
        IN_VMEM,
        pl.BlockSpec((1, 2, width), lambda i, where: (block_row(i, where), 0, column // width)),
    ]
    operands += [train, factor]
    return pl.pallas_call(
        lambda where, *refs: score_kernel(n, where, *refs),
        grid_spec=pltpu.PrefetchScalarGridSpec(
            num_scalar_prefetch=1,
            grid=(n,),
            in_specs=in_specs,
            out_specs=pl.BlockSpec(
                (rows, width), lambda i, where: (block_row(i, where), column // width)
            ),
        ),
        out_shape=jax.ShapeDtypeStruct(total, jnp.float32),
        input_output_aliases=aliases,
        compiler_params=pltpu.CompilerParams(vmem_limit_bytes=20 * 2**20),
        cost_estimate=pl.CostEstimate(
            flops=2 * n * rows * width * 4096,
            bytes_accessed=n * rows * width * 4,
            transcendentals=0,
        ),
    )(where, *operands)


def on_device(train_features, query_features, precond, example_weight, select):
    rows, cols = query_features.shape
    where = jnp.stack([lax.axis_index("y"), lax.axis_index("c")]).astype(jnp.int32)

    pieces = train_features.reshape(16, -1, cols)
    starts = [sum(WIDTHS[:n]) for n in range(len(WIDTHS))]
    cuts = [pieces[:, s : s + w] for s, w in zip(starts, WIDTHS)]

    p0 = lax.all_to_all(
        split_quarter(where, precond, cols), PB, split_axis=0, concat_axis=0, tiled=True
    )
    spread = jnp.broadcast_to(query_features[None], (8, rows, cols))
    q_own = lax.all_to_all(spread, ("z", "xl"), split_axis=0, concat_axis=0, tiled=True)
    p1 = shift(p0, 1)
    p3 = shift(p0, -1)
    p2 = shift(p0, 2)
    q_other = swap(q_own)
    tiles = conditioned_tiles(where, (p0, p1, p2, p3), q_own, q_other)

    plane = lax.all_to_all(tiles, PLANE, split_axis=0, concat_axis=0, tiled=True)
    plane = plane.reshape(2, 8, rows, cols)
    o0, o1 = plane[0], plane[1]
    a0 = shift(o0, 1)
    b1 = shift(o1, -1)
    a1 = shift(o1, 1)
    b0 = shift(o0, -1)
    f0 = shift(a0, 1)
    f1 = shift(b1, -1)

    def unit(x, offset, xh):
        return (x, swap(x), offset, xh)

    groups = [
        [unit(o0, 0, 0), unit(o1, 0, 1)],
        [unit(a0, 3, 0), unit(b1, 1, 1), unit(a1, 3, 1), unit(b0, 1, 0)],
        [unit(f0, 2, 0), unit(f1, 2, 1)],
    ]
    trains = []
    for cut in cuts:
        trains.append(lax.all_to_all(cut, PB, split_axis=0, concat_axis=0, tiled=True))
    factor = (
        jnp.repeat(select.astype(jnp.float32), BLK, axis=1)
        * (example_weight * (16 * cols) ** (-0.5))[None, :]
    ).reshape(8, 2, -1)
    out = None
    total = (2048, sum(WIDTHS))
    for train, start in zip(trains, starts):
        for group in groups:
            out = scores(where, group, train, factor, start, total, out)
    return out


def solution(mesh):
    fine = Mesh(mesh.devices.reshape(4, 2, 4, 2, 2), ("y", "xh", "z", "xl", "c"))
    ex, pb, both = ("y", "xh"), PB, ("y", "xh", *PB)
    placed = (P(ex, pb), P(ex, pb), P(pb, None), P(both), P(None, both))

    return jax.shard_map(on_device, mesh=fine, in_specs=placed, out_specs=P(None, both), check_vma=False)
```

time: 384 us -> 244 us (0.64)
  waiting for transfers between devices: 221 us -> 113 us
  blocking collectives: 97.5 us -> 12.3 us
  Pallas kernels: 0 us -> 51.2 us
  starting transfers between devices: 7.52 us -> 43.4 us
  matrix products: 26.2 us -> 0 us
  between operations: 13.4 us -> 0.13 us
  local copies, waits for them, and re-layouts: 17.3 us -> 22.9 us
    psum x1 -> x0, blocking collectives: 97.5 us -> none  [on_device(): lax.psum(jnp.dot(query_features, precond, preferred_element_type=jnp.floa...]
    all_to_all x1 -> x4, waiting for transfers between devices: 150 us -> 73 us  [the longest x2 35.5 us: on_device(): lax.all_to_all(cut, PB, split_axis=0, concat_axis=0, tiled=True)]
    all_gather x1 -> x0, waiting for transfers between devices: 70.8 us -> none  [on_device(): lax.all_gather(gathered, 'ex', axis=0, tiled=True)]
    pallas_call x0 -> x8, Pallas kernels: none -> 51.2 us  [the longest x6 47.7 us: scores(): pl.pallas_call(lambda where, *refs: score_kernel(n, where, *refs), grid_s...]
    ppermute x0 -> x18, waiting for transfers between devices: none -> 40.4 us  [the longest x9 40.4 us: shift(): return lax.ppermute(x, 'y', [(i, (i + by) % 4) for i in range(4)])]
    dot_general x2 -> x0, matrix products: 26.2 us -> none  [the longest x1 22.6 us: tile_product(): lax.dot_general(portion, train_tile, (((1,), (1,)), ((), ())), preferred_...]
    ppermute x0 -> x18, starting transfers between devices: none -> 19.2 us  [the longest x9 13.4 us: shift(): return lax.ppermute(x, 'y', [(i, (i + by) % 4) for i in range(4)])]
    all_to_all x1 -> x4, starting transfers between devices: 7.52 us -> 24.2 us  [the longest x2 11.8 us: on_device(): lax.all_to_all(cut, PB, split_axis=0, concat_axis=0, tiled=True)]
  transfers between devices with their start and end apart: 2 -> 22, of which waited for: 2 -> 6; matrix products, arithmetic and copies ran while one was open for 3% -> 4% of each run, Pallas kernels for 0% -> 13%
where the time goes in v1:
time: 244 us; the launch traced here: 243 us
  waiting for transfers between devices  113 us (46%)
  Pallas kernels  51.2 us (21%)
  starting transfers between devices  43.4 us (18%)
  local copies, waits for them, and re-layouts  22.9 us (9%)
  blocking collectives  12.3 us (5%)
    pallas_call x6, Pallas kernels, scores(): pl.pallas_call(lambda where, *refs: score_kernel(n, where, *refs), grid_s...  47.7 us
    ppermute x9, waiting for transfers between devices, shift(): return lax.ppermute(x, 'y', [(i, (i + by) % 4) for i in range(4)])  40.4 us
    all_to_all x2, waiting for transfers between devices, on_device(): lax.all_to_all(cut, PB, split_axis=0, concat_axis=0, tiled=True)  35.5 us
    all_to_all x1, waiting for transfers between devices, on_device(): lax.all_to_all(tiles, PLANE, split_axis=0, concat_axis=0, tiled=True)  22.9 us
    all_to_all x1, waiting for transfers between devices, on_device(): lax.all_to_all(spread, ('z', 'xl'), split_axis=0, concat_axis=0, tiled=True)  14.5 us
    ppermute x9, starting transfers between devices, shift(): return lax.ppermute(x, 'y', [(i, (i + by) % 4) for i in range(4)])  13.4 us
    all_to_all x1, blocking collectives, on_device(): lax.all_to_all(split_quarter(where, precond, cols), PB, split_axis=0, con...  12.3 us
    all_to_all x2, starting transfers between devices, on_device(): lax.all_to_all(cut, PB, split_axis=0, concat_axis=0, tiled=True)  11.8 us
  transfers between devices with their start and end apart: 22, of which 6 were waited for; matrix products, arithmetic and copies ran while one was open for 4% of the time, Pallas kernels for 13%

profile of v1, /device:TPU:1, one launch (start us, length us, event | category | flops | bytes accessed | tf_op | source)
XLA Modules:
  0.0 243.4 jit_solution(13283051119508622025)
XLA Ops:
  0.0 1.9 broadcast_in_dim.4
  1.9 6.8 %all-to-all-start.1 = ((bf16[8,256,256]{2,1,0:T(8,128)(2,1)}), bf16[8,256,256]{2,1,0:T(8,128)(2,1)S(1)}, u32[]{:S(2)}, u32[]{:S(2)}) async-start(bf16[8,256,256]{2,1,0:T(8,128)(2,1)} %broadcast_in_dim.4), calls=%async_computation.1 | async-start | bytes 2097152 | tf_op jit(solution)/shard_map/all_to_all | solution.py:154
  8.7 14.5 %all-to-all-done.1.own = bf16[8,256,256]{2,1,0:T(8,128)(2,1)S(1)} async-done(((bf16[8,256,256]{2,1,0:T(8,128)(2,1)}), bf16[8,256,256]{2,1,0:T(8,128)(2,1)S(1)}, u32[]{:S(2)}, u32[]{:S(2)}) %all-to-all-start.1) | async-done | bytes 1048608 | tf_op jit(solution)/shard_map/all_to_all | solution.py:154
  23.3 2.1 collective-permute-start.3
  25.5 1.6 copy-done.10
  27.0 0.6 shard_map.55
  27.6 12.3 %all_to_all.25.p0 = bf16[16,64,256]{2,1,0:T(8,128)(2,1)S(1)} all-to-all(bf16[16,64,256]{2,1,0:T(8,128)(2,1)S(1)} %shard_map.55), channel_id=1, replica_groups=mesh['y'=4,'xh'=2,'z'=4,'xl'=2,'c'=2] {'z','xl','c'}, dimensions={0} | all-to-all | bytes 1048576 | tf_op jit(solution)/shard_map/all_to_all | solution.py:150
  39.9 1.3 collective-permute-start
  41.2 2.6 %collective-permute-start.1 = (bf16[16,64,256]{2,1,0:T(8,128)(2,1)S(1)}, bf16[16,64,256]{2,1,0:T(8,128)(2,1)S(1)}, u32[]{:S(2)}, u32[]{:S(2)}) collective-permute-start(bf16[16,64,256]{2,1,0:T(8,128)(2,1)S(1)} %all_to_all.25.p0), channel_id=1, source_target_pairs={{0,64},{32,96},{64,0},{96,32},{1,65},{33,97},{65,1},{97,33},{2,66}... | collective-permute-start | bytes 1572872 | tf_op jit(solution)/shard_map/ppermute | solution.py:18
  43.9 1.1 collective-permute-start.2
  44.9 8.6 %collective-permute-done.p1 = bf16[16,64,256]{2,1,0:T(8,128)(2,1)S(1)} collective-permute-done((bf16[16,64,256]{2,1,0:T(8,128)(2,1)S(1)}, bf16[16,64,256]{2,1,0:T(8,128)(2,1)S(1)}, u32[]{:S(2)}, u32[]{:S(2)}) %collective-permute-start) | collective-permute-done | bytes 524320 | tf_op jit(solution)/shard_map/ppermute | solution.py:18
  53.5 12.4 %collective-permute-done.1.p2 = bf16[16,64,256]{2,1,0:T(8,128)(2,1)S(1)} collective-permute-done((bf16[16,64,256]{2,1,0:T(8,128)(2,1)S(1)}, bf16[16,64,256]{2,1,0:T(8,128)(2,1)S(1)}, u32[]{:S(2)}, u32[]{:S(2)}) %collective-permute-start.1) | collective-permute-done | bytes 524320 | tf_op jit(solution)/shard_map/ppermute | solution.py:18
  65.9 2.9 %shard_map.56 = bf16[16,256,256]{2,1,0:T(8,128)(2,1)} custom-call(s32[2]{0:T(128)S(1)} %pad_add_fusion.where, bf16[16,64,256]{2,1,0:T(8,128)(2,1)S(1)} %all_to_all.25.p0, bf16[16,64,256]{2,1,0:T(8,128)(2,1)S(1)} %collective-permute-done.p1, bf16[16,64,256]{2,1,0:T(8,128)(2,1)S(1)} %collective-permute-done.1.p2, ...), custom_call_target="tpu_custom_call" | custom-call | tf_op jit(solution)/shard_map/pallas_call | solution.py:66
  68.8 5.6 %all-to-all-start.2 = ((bf16[16,256,256]{2,1,0:T(8,128)(2,1)}), bf16[16,256,256]{2,1,0:T(8,128)(2,1)S(1)}, u32[]{:S(2)}, u32[]{:S(2)}) async-start(bf16[16,256,256]{2,1,0:T(8,128)(2,1)} %shard_map.56), calls=%async_computation.2 | async-start | bytes 4194304 | tf_op jit(solution)/shard_map/all_to_all | solution.py:161
  74.4 6.1 %slice.20 = bf16[16,768,256]{2,1,0:T(8,128)(2,1)} slice(bf16[16,1024,256]{2,1,0:T(8,128)(2,1)} %bitcast.3), slice={[0:16], [0:768], [0:256]} | slice | bytes 12582912 | tf_op jit(solution)/shard_map/slice | solution.py:148
  80.4 22.9 %all-to-all-done.2 = bf16[16,256,256]{2,1,0:T(8,128)(2,1)S(1)} async-done(((bf16[16,256,256]{2,1,0:T(8,128)(2,1)}), bf16[16,256,256]{2,1,0:T(8,128)(2,1)S(1)}, u32[]{:S(2)}, u32[]{:S(2)}) %all-to-all-start.2) | async-done | bytes 2097184 | tf_op jit(solution)/shard_map/all_to_all | solution.py:161
  103.3 7.3 %all-to-all-start.3 = ((bf16[16,768,256]{2,1,0:T(8,128)(2,1)}), bf16[16,768,256]{2,1,0:T(8,128)(2,1)}, u32[]{:S(2)}, u32[]{:S(2)}) async-start(bf16[16,768,256]{2,1,0:T(8,128)(2,1)} %slice.20), calls=%async_computation.3 | async-start | bytes 12582912 | tf_op jit(solution)/shard_map/all_to_all | solution.py:181
  110.6 1.1 fusion
  111.7 0.1 collective-permute-start.16
  111.9 0.9 collective-permute-start.4
  112.8 0.6 collective-permute-start.17
  113.4 2.2 collective-permute-start.7
  115.6 1.0 copy-done
  116.6 2.7 %collective-permute-start.14 = (bf16[8,256,256]{2,1,0:T(8,128)(2,1)}, bf16[8,256,256]{2,1,0:T(8,128)(2,1)}, u32[]{:S(2)}, u32[]{:S(2)}) collective-permute-start(bf16[8,256,256]{2,1,0:T(8,128)(2,1)} %get-tuple-element.6.refs_0_), channel_id=1, source_target_pairs={{0,96},{32,0},{64,32},{96,64},{1,97},{33,1},{65,33},{97,65},{2,98}... | collective-permute-start | bytes 3145736 | tf_op jit(solution)/shard_map/ppermute | solution.py:18
  119.3 19.5 %collective-permute-done.4.refs_0_ = bf16[8,256,256]{2,1,0:T(8,128)(2,1)} collective-permute-done((bf16[8,256,256]{2,1,0:T(8,128)(2,1)}, bf16[8,256,256]{2,1,0:T(8,128)(2,1)}, u32[]{:S(2)}, u32[]{:S(2)}) %collective-permute-start.4) | collective-permute-done | bytes 1048608 | tf_op jit(solution)/shard_map/ppermute | solution.py:18
  138.7 1.5 collective-permute-start.10
  140.2 1.0 copy-done.3
  141.2 2.7 %collective-permute-start.8 = (bf16[8,256,256]{2,1,0:T(8,128)(2,1)}, bf16[8,256,256]{2,1,0:T(8,128)(2,1)}, u32[]{:S(2)}, u32[]{:S(2)}) collective-permute-start(bf16[8,256,256]{2,1,0:T(8,128)(2,1)} %collective-permute-done.7.refs_2_), channel_id=1, source_target_pairs={{0,96},{32,0},{64,32},{96,64},{1,97},{33,1},{65,33},{97,65},{2,98}... | collective-permute-start | bytes 3145736 | tf_op jit(solution)/shard_map/ppermute | solution.py:18
  143.9 3.2 %slice.21 = bf16[16,256,256]{2,1,0:T(8,128)(2,1)} slice(bf16[16,1024,256]{2,1,0:T(8,128)(2,1)} %bitcast.4), slice={[0:16], [768:1024], [0:256]} | slice | bytes 4194304 | tf_op jit(solution)/shard_map/slice | solution.py:148
  147.1 35.5 %all-to-all-done.3.refs_4_.refs_9_.refs_5_ = bf16[16,768,256]{2,1,0:T(8,128)(2,1)} async-done(((bf16[16,768,256]{2,1,0:T(8,128)(2,1)}), bf16[16,768,256]{2,1,0:T(8,128)(2,1)}, u32[]{:S(2)}, u32[]{:S(2)}) %all-to-all-start.3) | async-done | bytes 6291488 | tf_op jit(solution)/shard_map/all_to_all | solution.py:181
  182.6 4.5 %all-to-all-start.4 = ((bf16[16,256,256]{2,1,0:T(8,128)(2,1)}), bf16[16,256,256]{2,1,0:T(8,128)(2,1)S(1)}, u32[]{:S(2)}, u32[]{:S(2)}) async-start(bf16[16,256,256]{2,1,0:T(8,128)(2,1)} %slice.21), calls=%async_computation.4 | async-start | bytes 4194304 | tf_op jit(solution)/shard_map/all_to_all | solution.py:181
  187.1 0.3 collective-permute-start.11
  187.4 0.3 collective-permute-start.13
  187.7 0.2 collective-permute-start.15
  188.1 0.4 collective-permute-start.6
  188.5 0.3 collective-permute-start.9
  188.8 1.2 copy-done.1
  190.1 1.2 copy-done.4
  191.3 8.2 %shard_map.57.refs_8_ = f32[2048,1024]{1,0:T(8,128)} custom-call(s32[2]{0:T(128)S(1)} %pad_add_fusion.where, bf16[8,256,256]{2,1,0:T(8,128)(2,1)} %get-tuple-element.6.refs_0_, bf16[8,256,256]{2,1,0:T(8,128)(2,1)S(1)} %copy-done.1, bf16[8,256,256]{2,1,0:T(8,128)(2,1)S(1)} %get-tuple-element.5.refs_2_, bf16[8,256,256]{2,1,0:T(8,128)(2,1)S(1)} %copy-done.4, ...), custom_call_target="tpu_custom_call" | custom-call | flops 3221225472 | bytes 1572864 | tf_op jit(solution)/shard_map/pallas_call | solution.py:121
  199.5 14.3 %shard_map.58.refs_4_ = f32[2048,1024]{1,0:T(8,128)} custom-call(s32[2]{0:T(128)S(1)} %pad_add_fusion.where, bf16[8,256,256]{2,1,0:T(8,128)(2,1)} %collective-permute-done.4.refs_0_, bf16[8,256,256]{2,1,0:T(8,128)(2,1)} %collective-permute-done.10.refs_1_, bf16[8,256,256]{2,1,0:T(8,128)(2,1)} %collective-permute-done.7.refs_2_, ...), custom_call_target="tpu_custom_call", output_to_operand_aliasing={{}: (9, {})} | custom-call | flops 6442450944 | bytes 3145728 | tf_op jit(solution)/shard_map/pallas_call | solution.py:121
  213.8 8.6 %shard_map.59.refs_4_ = f32[2048,1024]{1,0:T(8,128)} custom-call(s32[2]{0:T(128)S(1)} %pad_add_fusion.where, bf16[8,256,256]{2,1,0:T(8,128)(2,1)} %collective-permute-done.5.refs_0_, bf16[8,256,256]{2,1,0:T(8,128)(2,1)S(1)} %collective-permute-done.6.refs_1_, bf16[8,256,256]{2,1,0:T(8,128)(2,1)} %collective-permute-done.8.refs_2_, ...), custom_call_target="tpu_custom_call", output_to_operand_aliasing={{}: (5, {})} | custom-call | flops 3221225472 | bytes 1572864 | tf_op jit(solution)/shard_map/pallas_call | solution.py:121
  222.4 1.0 copy-done.6
  223.4 1.0 copy-done.8
  224.4 1.2 copy-done.2
  225.6 1.2 copy-done.5
  226.9 4.0 %shard_map.60.refs_8_ = f32[2048,1024]{1,0:T(8,128)} custom-call(s32[2]{0:T(128)S(1)} %pad_add_fusion.where, bf16[8,256,256]{2,1,0:T(8,128)(2,1)} %get-tuple-element.6.refs_0_, bf16[8,256,256]{2,1,0:T(8,128)(2,1)S(1)} %copy-done.2, bf16[8,256,256]{2,1,0:T(8,128)(2,1)S(1)} %get-tuple-element.5.refs_2_, ...), custom_call_target="tpu_custom_call", output_to_operand_aliasing={{}: (5, {})} | custom-call | flops 1073741824 | bytes 524288 | tf_op jit(solution)/shard_map/pallas_call | solution.py:121
  230.9 8.1 %shard_map.61.refs_4_ = f32[2048,1024]{1,0:T(8,128)} custom-call(s32[2]{0:T(128)S(1)} %pad_add_fusion.where, bf16[8,256,256]{2,1,0:T(8,128)(2,1)} %collective-permute-done.4.refs_0_, bf16[8,256,256]{2,1,0:T(8,128)(2,1)} %collective-permute-done.10.refs_1_, bf16[8,256,256]{2,1,0:T(8,128)(2,1)} %collective-permute-done.7.refs_2_, ...), custom_call_target="tpu_custom_call", output_to_operand_aliasing={{}: (9, {})} | custom-call | flops 2147483648 | bytes 1048576 | tf_op jit(solution)/shard_map/pallas_call | solution.py:121
  239.0 4.4 %shard_map.62 = f32[2048,1024]{1,0:T(8,128)} custom-call(s32[2]{0:T(128)S(1)} %pad_add_fusion.where, bf16[8,256,256]{2,1,0:T(8,128)(2,1)} %collective-permute-done.5.refs_0_, bf16[8,256,256]{2,1,0:T(8,128)(2,1)S(1)} %copy-done.7, bf16[8,256,256]{2,1,0:T(8,128)(2,1)} %collective-permute-done.8.refs_2_, ...), custom_call_target="tpu_custom_call", output_to_operand_aliasing={{}: (5, {})} | custom-call | flops 1073741824 | bytes 524288 | tf_op jit(solution)/shard_map/pallas_call | solution.py:121
  (42 shorter events, 0.4 us)
Async XLA Ops:
  1.9 21.3 %all-to-all-start.1 = ((bf16[8,256,256]{2,1,0:T(8,128)(2,1)}), bf16[8,256,256]{2,1,0:T(8,128)(2,1)S(1)}, u32[]{:S(2)}, u32[]{:S(2)}) async-start(bf16[8,256,256]{2,1,0:T(8,128)(2,1)} %broadcast_in_dim.4), calls=%async_computation.1 | async-start | bytes 2097152 | tf_op jit(solution)/shard_map/all_to_all | solution.py:154
  23.3 42.6 %collective-permute-start.3 = (bf16[8,256,256]{2,1,0:T(8,128)(2,1)S(1)}, bf16[8,256,256]{2,1,0:T(8,128)(2,1)S(1)}, u32[]{:S(2)}, u32[]{:S(2)}) collective-permute-start(bf16[8,256,256]{2,1,0:T(8,128)(2,1)S(1)} %all-to-all-done.1.own), channel_id=1, source_target_pairs={{0,1},{1,0},{2,3},{3,2},{4,5},{5,4},{6,7},{7,6},{8,9},{9,8},{10,11... | collective-permute-start | bytes 3145736 | tf_op jit(solution)/shard_map/ppermute | solution.py:22
  25.5 1.6 copy-start.10
  39.9 13.5 %collective-permute-start = (bf16[16,64,256]{2,1,0:T(8,128)(2,1)S(1)}, bf16[16,64,256]{2,1,0:T(8,128)(2,1)S(1)}, u32[]{:S(2)}, u32[]{:S(2)}) collective-permute-start(bf16[16,64,256]{2,1,0:T(8,128)(2,1)S(1)} %all_to_all.25.p0), channel_id=1, source_target_pairs={{0,32},{32,64},{64,96},{96,0},{1,33},{33,65},{65,97},{97,1},{2,34}... | collective-permute-start | bytes 1572872 | tf_op jit(solution)/shard_map/ppermute | solution.py:18
  41.2 24.6 %collective-permute-start.1 = (bf16[16,64,256]{2,1,0:T(8,128)(2,1)S(1)}, bf16[16,64,256]{2,1,0:T(8,128)(2,1)S(1)}, u32[]{:S(2)}, u32[]{:S(2)}) collective-permute-start(bf16[16,64,256]{2,1,0:T(8,128)(2,1)S(1)} %all_to_all.25.p0), channel_id=1, source_target_pairs={{0,64},{32,96},{64,0},{96,32},{1,65},{33,97},{65,1},{97,33},{2,66}... | collective-permute-start | bytes 1572872 | tf_op jit(solution)/shard_map/ppermute | solution.py:18
  43.9 22.0 %collective-permute-start.2 = (bf16[16,64,256]{2,1,0:T(8,128)(2,1)S(1)}, bf16[16,64,256]{2,1,0:T(8,128)(2,1)S(1)}, u32[]{:S(2)}, u32[]{:S(2)}) collective-permute-start(bf16[16,64,256]{2,1,0:T(8,128)(2,1)S(1)} %all_to_all.25.p0), channel_id=1, source_target_pairs={{0,96},{32,0},{64,32},{96,64},{1,97},{33,1},{65,33},{97,65},{2,98}... | collective-permute-start | bytes 1572872 | tf_op jit(solution)/shard_map/ppermute | solution.py:18
  68.8 34.5 %all-to-all-start.2 = ((bf16[16,256,256]{2,1,0:T(8,128)(2,1)}), bf16[16,256,256]{2,1,0:T(8,128)(2,1)S(1)}, u32[]{:S(2)}, u32[]{:S(2)}) async-start(bf16[16,256,256]{2,1,0:T(8,128)(2,1)} %shard_map.56), calls=%async_computation.2 | async-start | bytes 4194304 | tf_op jit(solution)/shard_map/all_to_all | solution.py:161
  103.3 79.3 %all-to-all-start.3 = ((bf16[16,768,256]{2,1,0:T(8,128)(2,1)}), bf16[16,768,256]{2,1,0:T(8,128)(2,1)}, u32[]{:S(2)}, u32[]{:S(2)}) async-start(bf16[16,768,256]{2,1,0:T(8,128)(2,1)} %slice.20), calls=%async_computation.3 | async-start | bytes 12582912 | tf_op jit(solution)/shard_map/all_to_all | solution.py:181
  110.6 77.3 %copy-start.11 = (s32[16,8]{0,1:T(8,128)S(1)}, s32[16,8]{0,1:T(8,128)}, u32[]{:S(2)}) copy-start(s32[16,8]{0,1:T(8,128)} %param.9) | copy-start | bytes 1540
  110.6 77.5 %copy-start.12 = (f32[1024]{0:T(1024)S(1)}, f32[1024]{0:T(1024)}, u32[]{:S(2)}) copy-start(f32[1024]{0:T(1024)} %param.8) | copy-start | bytes 12292
  111.7 3.9 %collective-permute-start.16 = (bf16[8,256,256]{2,1,0:T(8,128)(2,1)}, bf16[8,256,256]{2,1,0:T(8,128)(2,1)S(1)}, u32[]{:S(2)}, u32[]{:S(2)}) collective-permute-start(bf16[8,256,256]{2,1,0:T(8,128)(2,1)} %get-tuple-element.6.refs_0_), channel_id=1, source_target_pairs={{0,1},{1,0},{2,3},{3,2},{4,5},{5,4},{6,7},{7,6},{8,9},{9,8},{10,11... | collective-permute-start | bytes 3145736 | tf_op jit(solution)/shard_map/ppermute | solution.py:22
  111.9 26.8 %collective-permute-start.4 = (bf16[8,256,256]{2,1,0:T(8,128)(2,1)}, bf16[8,256,256]{2,1,0:T(8,128)(2,1)}, u32[]{:S(2)}, u32[]{:S(2)}) collective-permute-start(bf16[8,256,256]{2,1,0:T(8,128)(2,1)} %get-tuple-element.6.refs_0_), channel_id=1, source_target_pairs={{0,32},{32,64},{64,96},{96,0},{1,33},{33,65},{65,97},{97,1},{2,34}... | collective-permute-start | bytes 3145736 | tf_op jit(solution)/shard_map/ppermute | solution.py:18
  112.8 27.4 %collective-permute-start.17 = (bf16[8,256,256]{2,1,0:T(8,128)(2,1)S(1)}, bf16[8,256,256]{2,1,0:T(8,128)(2,1)S(1)}, u32[]{:S(2)}, u32[]{:S(2)}) collective-permute-start(bf16[8,256,256]{2,1,0:T(8,128)(2,1)S(1)} %get-tuple-element.5.refs_2_), channel_id=1, source_target_pairs={{0,1},{1,0},{2,3},{3,2},{4,5},{5,4},{6,7},{7,6},{8,9},{9,8},{10,11... | collective-permute-start | bytes 3145736 | tf_op jit(solution)/shard_map/ppermute | solution.py:22
  113.4 27.8 %collective-permute-start.7 = (bf16[8,256,256]{2,1,0:T(8,128)(2,1)S(1)}, bf16[8,256,256]{2,1,0:T(8,128)(2,1)}, u32[]{:S(2)}, u32[]{:S(2)}) collective-permute-start(bf16[8,256,256]{2,1,0:T(8,128)(2,1)S(1)} %get-tuple-element.5.refs_2_), channel_id=1, source_target_pairs={{0,96},{32,0},{64,32},{96,64},{1,97},{33,1},{65,33},{97,65},{2,98}... | collective-permute-start | bytes 3145736 | tf_op jit(solution)/shard_map/ppermute | solution.py:18
  115.6 71.5 %collective-permute-start.12 = (bf16[8,256,256]{2,1,0:T(8,128)(2,1)S(1)}, bf16[8,256,256]{2,1,0:T(8,128)(2,1)}, u32[]{:S(2)}, u32[]{:S(2)}) collective-permute-start(bf16[8,256,256]{2,1,0:T(8,128)(2,1)S(1)} %get-tuple-element.5.refs_2_), channel_id=1, source_target_pairs={{0,32},{32,64},{64,96},{96,0},{1,33},{33,65},{65,97},{97,1},{2,34}... | collective-permute-start | bytes 3145736 | tf_op jit(solution)/shard_map/ppermute | solution.py:18
  115.6 1.0 copy-start
  116.6 70.8 %collective-permute-start.14 = (bf16[8,256,256]{2,1,0:T(8,128)(2,1)}, bf16[8,256,256]{2,1,0:T(8,128)(2,1)}, u32[]{:S(2)}, u32[]{:S(2)}) collective-permute-start(bf16[8,256,256]{2,1,0:T(8,128)(2,1)} %get-tuple-element.6.refs_0_), channel_id=1, source_target_pairs={{0,96},{32,0},{64,32},{96,64},{1,97},{33,1},{65,33},{97,65},{2,98}... | collective-permute-start | bytes 3145736 | tf_op jit(solution)/shard_map/ppermute | solution.py:18
  138.7 49.0 %collective-permute-start.10 = (bf16[8,256,256]{2,1,0:T(8,128)(2,1)}, bf16[8,256,256]{2,1,0:T(8,128)(2,1)}, u32[]{:S(2)}, u32[]{:S(2)}) collective-permute-start(bf16[8,256,256]{2,1,0:T(8,128)(2,1)} %collective-permute-done.4.refs_0_), channel_id=1, source_target_pairs={{0,1},{1,0},{2,3},{3,2},{4,5},{5,4},{6,7},{7,6},{8,9},{9,8},{10,11... | collective-permute-start | bytes 3145736 | tf_op jit(solution)/shard_map/ppermute | solution.py:22
  140.2 1.0 copy-start.3
  141.2 46.9 %collective-permute-start.5 = (bf16[8,256,256]{2,1,0:T(8,128)(2,1)}, bf16[8,256,256]{2,1,0:T(8,128)(2,1)}, u32[]{:S(2)}, u32[]{:S(2)}) collective-permute-start(bf16[8,256,256]{2,1,0:T(8,128)(2,1)} %collective-permute-done.4.refs_0_), channel_id=1, source_target_pairs={{0,32},{32,64},{64,96},{96,0},{1,33},{33,65},{65,97},{97,1},{2,34}... | collective-permute-start | bytes 3145736 | tf_op jit(solution)/shard_map/ppermute | solution.py:18
  141.2 47.3 %collective-permute-start.8 = (bf16[8,256,256]{2,1,0:T(8,128)(2,1)}, bf16[8,256,256]{2,1,0:T(8,128)(2,1)}, u32[]{:S(2)}, u32[]{:S(2)}) collective-permute-start(bf16[8,256,256]{2,1,0:T(8,128)(2,1)} %collective-permute-done.7.refs_2_), channel_id=1, source_target_pairs={{0,96},{32,0},{64,32},{96,64},{1,97},{33,1},{65,33},{97,65},{2,98}... | collective-permute-start | bytes 3145736 | tf_op jit(solution)/shard_map/ppermute | solution.py:18
  182.6 41.8 %all-to-all-start.4 = ((bf16[16,256,256]{2,1,0:T(8,128)(2,1)}), bf16[16,256,256]{2,1,0:T(8,128)(2,1)S(1)}, u32[]{:S(2)}, u32[]{:S(2)}) async-start(bf16[16,256,256]{2,1,0:T(8,128)(2,1)} %slice.21), calls=%async_computation.4 | async-start | bytes 4194304 | tf_op jit(solution)/shard_map/all_to_all | solution.py:181
  187.1 12.4 %collective-permute-start.11 = (bf16[8,256,256]{2,1,0:T(8,128)(2,1)}, bf16[8,256,256]{2,1,0:T(8,128)(2,1)}, u32[]{:S(2)}, u32[]{:S(2)}) collective-permute-start(bf16[8,256,256]{2,1,0:T(8,128)(2,1)} %collective-permute-done.7.refs_2_), channel_id=1, source_target_pairs={{0,1},{1,0},{2,3},{3,2},{4,5},{5,4},{6,7},{7,6},{8,9},{9,8},{10,11... | collective-permute-start | bytes 3145736 | tf_op jit(solution)/shard_map/ppermute | solution.py:22
  187.4 12.1 %collective-permute-start.13 = (bf16[8,256,256]{2,1,0:T(8,128)(2,1)}, bf16[8,256,256]{2,1,0:T(8,128)(2,1)}, u32[]{:S(2)}, u32[]{:S(2)}) collective-permute-start(bf16[8,256,256]{2,1,0:T(8,128)(2,1)} %collective-permute-done.12.refs_4_), channel_id=1, source_target_pairs={{0,1},{1,0},{2,3},{3,2},{4,5},{5,4},{6,7},{7,6},{8,9},{9,8},{10,11... | collective-permute-start | bytes 3145736 | tf_op jit(solution)/shard_map/ppermute | solution.py:22
  187.7 11.8 %collective-permute-start.15 = (bf16[8,256,256]{2,1,0:T(8,128)(2,1)}, bf16[8,256,256]{2,1,0:T(8,128)(2,1)}, u32[]{:S(2)}, u32[]{:S(2)}) collective-permute-start(bf16[8,256,256]{2,1,0:T(8,128)(2,1)} %collective-permute-done.14.refs_6_), channel_id=1, source_target_pairs={{0,1},{1,0},{2,3},{3,2},{4,5},{5,4},{6,7},{7,6},{8,9},{9,8},{10,11... | collective-permute-start | bytes 3145736 | tf_op jit(solution)/shard_map/ppermute | solution.py:22
  188.1 25.7 %collective-permute-start.6 = (bf16[8,256,256]{2,1,0:T(8,128)(2,1)}, bf16[8,256,256]{2,1,0:T(8,128)(2,1)S(1)}, u32[]{:S(2)}, u32[]{:S(2)}) collective-permute-start(bf16[8,256,256]{2,1,0:T(8,128)(2,1)} %collective-permute-done.5.refs_0_), channel_id=1, source_target_pairs={{0,1},{1,0},{2,3},{3,2},{4,5},{5,4},{6,7},{7,6},{8,9},{9,8},{10,11... | collective-permute-start | bytes 3145736 | tf_op jit(solution)/shard_map/ppermute | solution.py:22
  188.5 25.3 %collective-permute-start.9 = (bf16[8,256,256]{2,1,0:T(8,128)(2,1)}, bf16[8,256,256]{2,1,0:T(8,128)(2,1)S(1)}, u32[]{:S(2)}, u32[]{:S(2)}) collective-permute-start(bf16[8,256,256]{2,1,0:T(8,128)(2,1)} %collective-permute-done.8.refs_2_), channel_id=1, source_target_pairs={{0,1},{1,0},{2,3},{3,2},{4,5},{5,4},{6,7},{7,6},{8,9},{9,8},{10,11... | collective-permute-start | bytes 3145736 | tf_op jit(solution)/shard_map/ppermute | solution.py:22
  188.8 1.2 copy-start.1
  190.0 1.2 copy-start.4
  222.4 1.0 copy-start.6
  223.4 1.0 copy-start.8
  224.4 1.2 copy-start.2
  225.6 1.2 copy-start.5
  230.9 8.2 %copy-start.7 = (bf16[8,256,256]{2,1,0:T(8,128)(2,1)S(1)}, bf16[8,256,256]{2,1,0:T(8,128)(2,1)}, u32[]{:S(2)}) copy-start(bf16[8,256,256]{2,1,0:T(8,128)(2,1)} %copy-done.6) | copy-start | bytes 3145732
  230.9 8.2 %copy-start.9 = (bf16[8,256,256]{2,1,0:T(8,128)(2,1)S(1)}, bf16[8,256,256]{2,1,0:T(8,128)(2,1)}, u32[]{:S(2)}) copy-start(bf16[8,256,256]{2,1,0:T(8,128)(2,1)} %copy-done.8) | copy-start | bytes 3145732

commit v2 on v0

v2 whole, which is shorter than its diff:
```python
import jax
import jax.numpy as jnp
from jax import lax
from jax.experimental import pallas as pl
from jax.experimental.pallas import tpu as pltpu
from jax.sharding import Mesh, PartitionSpec as P

BLK = 128
PB = ("z", "xl", "c")
WIDTHS = (160, 608, 256)

IN_VMEM = pl.BlockSpec(memory_space=pltpu.VMEM)
IN_SMEM = pl.BlockSpec(memory_space=pltpu.SMEM)
ANYWHERE = pl.BlockSpec(memory_space=pl.ANY)


def shift(x, by):
    return lax.ppermute(x, "y", [(i, (i + by) % 4) for i in range(4)])


def ring(x, axis):
    got = {0: x}
    for by in (1, 3, 2):
        got[by] = lax.ppermute(x, axis, [(i, (i + by) % 4) for i in range(4)])
    return [got[by] for by in range(4)]


def swap(x):
    return lax.ppermute(x, "c", [(0, 1), (1, 0)])


def split_kernel(where, p, out):
    cols = out.shape[2]
    for j in range(out.shape[0]):
        out[j] = p[:, j * cols : (j + 1) * cols]


def split_quarter(where, precond, cols):
    rows = precond.shape[0] // 4
    blocks = precond.shape[1] // cols
    return pl.pallas_call(
        split_kernel,
        grid_spec=pltpu.PrefetchScalarGridSpec(
            num_scalar_prefetch=1,
            grid=(1,),
            in_specs=[pl.BlockSpec((rows, precond.shape[1]), lambda i, where: (where[0], 0))],
            out_specs=pl.BlockSpec((blocks, rows, cols), lambda i, where: (0, 0, 0)),
        ),
        out_shape=jax.ShapeDtypeStruct((blocks, rows, cols), precond.dtype),
        compiler_params=pltpu.CompilerParams(vmem_limit_bytes=60 * 2**20),
    )(where, precond)


def stack_kernel(*refs):
    out, at = refs[-1], 0
    for ref in refs[:-1]:
        if len(ref.shape) == 2:
            out[at] = ref[...]
            at += 1
        else:
            out[at : at + ref.shape[0]] = ref[...]
            at += ref.shape[0]


def stack(*parts):
    count = sum(1 if x.ndim == 2 else x.shape[0] for x in parts)
    shape = (count, *parts[0].shape[-2:])
    return pl.pallas_call(
        stack_kernel,
        in_specs=[IN_VMEM] * len(parts),
        out_specs=IN_VMEM,
        out_shape=jax.ShapeDtypeStruct(shape, parts[0].dtype),
        compiler_params=pltpu.CompilerParams(vmem_limit_bytes=8 * 2**20),
    )(*parts)


def tile_kernel(where, *refs):
    p, q, (out, whole) = refs[:4], refs[4:-2], refs[-2:]
    y, core, z, xl = where[0], where[2], where[3], where[4]
    quarter = p[0].shape[1]
    for back in range(4):
        start = pl.multiple_of(lax.rem(y + 4 - back, 4) * quarter, quarter)
        whole[:, pl.ds(start, quarter), :] = p[back][...]
    acc = None
    for back in range(4):
        zz = lax.rem(z + 4 - back, 4)
        for half in range(2):
            side = core if half == 0 else 1 - core
            for flip in range(2):
                source = zz * 4 + (xl if flip == 0 else 1 - xl) * 2 + side
                part = jnp.dot(
                    q[half][2 * back + flip], whole[source], preferred_element_type=jnp.float32
                )
                acc = part if acc is None else acc + part
    tile = acc.astype(out.dtype)
    for k in range(out.shape[0]):
        out[k] = tile


def conditioned_tile(where, p, q):
    rows = q[0].shape[1]
    return pl.pallas_call(
        tile_kernel,
        in_specs=[IN_SMEM] + [IN_VMEM] * (len(p) + len(q)),
        out_specs=IN_VMEM,
        out_shape=jax.ShapeDtypeStruct((8, rows, rows), jnp.bfloat16),
        scratch_shapes=[pltpu.VMEM((16, rows, rows), jnp.bfloat16)],
        compiler_params=pltpu.CompilerParams(vmem_limit_bytes=12 * 2**20),
    )(where, *p, *q)


def score_kernel(places, widths, jobs, first, where, *refs):
    n, m = len(places), len(widths)
    units, trains, factor = refs[: 2 * n], refs[2 * n : 2 * n + m], refs[2 * n + m]
    held, rows_t, unit_sem, train_sem, out_sem = refs[-5 - len(jobs) : -len(jobs)]
    out, readies = refs[-6 - len(jobs)], refs[-len(jobs) :]
    y, xh, core = where[0], where[1], where[2]
    slots, rows = held.shape[0], held.shape[3]
    at = [sum(widths[:k]) for k in range(m + 1)]

    def load(k, slot, half):
        return pltpu.make_async_copy(
            units[2 * k + half], held.at[slot, half], unit_sem.at[slot, half]
        )

    fetches = [
        pltpu.make_async_copy(trains[k], rows_t.at[:, pl.ds(at[k], widths[k]), :], train_sem.at[k])
        for k in range(m)
    ]
    pending = list(range(m))
    for half in range(2):
        load(0, 0, half).start()
    for k in range(jobs[0][2], jobs[0][3]):
        fetches[k].start()
    for k in range(1, min(slots - 1, n)):
        for half in range(2):
            load(k, k, half).start()
    for k in range(m):
        if not jobs[0][2] <= k < jobs[0][3]:
            fetches[k].start()

    for number, (low, high, start, stop) in enumerate(jobs):
        left, width, ready = at[start], at[stop] - at[start], readies[number]
        for k in range(start, stop):
            if k in pending:
                pending.remove(k)
                fetches[k].wait()

        def store(row, lane):
            top = pl.multiple_of(row * rows, rows)
            return pltpu.make_async_copy(
                ready.at[lane],
                out.at[pl.ds(top, rows), pl.ds(first + left, width)],
                out_sem.at[number, lane],
            )

        @pl.loop(low, high)
        def _(j):
            for k in range(max(slots - 1, low + slots - 1), min(n, high + slots - 1)):

                @pl.when(j + slots - 1 == k)
                def _():
                    for half in range(2):
                        load(k, k % slots, half).start()

            slot = lax.rem(j, slots)
            offset, flip = places[low]
            for k in range(low + 1, high):
                offset = jnp.where(j == k, places[k][0], offset)
                flip = jnp.where(j == k, places[k][1], flip)
            for half in range(2):
                load(0, slot, half).wait()
            acc = None
            for half in range(2):
                side = core if half == 0 else 1 - core
                for s in range(8):
                    part = lax.dot_general(
                        held[slot, half, s],
                        rows_t[2 * s + side, left : left + width, :],
                        (((1,), (1,)), ((), ())),
                        preferred_element_type=jnp.float32,
                    )
                    acc = part if acc is None else acc + part
            row = lax.rem(y + offset, 4) * 2 + jnp.where(flip == 1, 1 - xh, xh)
            lane = lax.rem(j - low, 2)

            @pl.when(j >= low + 2)
            def _():
                store(row, lane).wait()

            for h in range(2):
                part = slice(h * BLK, (h + 1) * BLK)
                scale = factor[row, h : h + 1, first + left : first + left + width]
                ready[lane, part, :] = acc[part] * scale
            store(row, lane).start()

        for lane in range(min(2, high - low)):
            if number + 1 == len(jobs):
                store(0, lane).wait()

    for number, (low, high, start, stop) in enumerate(jobs[:-1]):
        for lane in range(min(2, high - low)):
            pltpu.make_async_copy(
                readies[number].at[lane],
                out.at[pl.ds(0, rows), pl.ds(first + at[start], at[stop] - at[start])],
                out_sem.at[number, lane],
            ).wait()


def scores(where, units, places, trains, jobs, factor, first, total, previous):
    widths = [train.shape[1] for train in trains]
    pieces, rows, cols = units[0].shape
    operands = [where, *units, *trains, factor]
    specs = [IN_SMEM] + [ANYWHERE] * (len(units) + len(trains)) + [IN_VMEM]
    aliases = {}
    if previous is not None:
        aliases = {len(operands): 0}
        specs.append(ANYWHERE)
        operands.append(previous)
    spans = [sum(widths[start:stop]) for _, _, start, stop in jobs]
    work = sum((job[1] - job[0]) * span for job, span in zip(jobs, spans))
    return pl.pallas_call(
        lambda *refs: score_kernel(places, widths, jobs, first, *refs),
        in_specs=specs,
        out_specs=ANYWHERE,
        out_shape=jax.ShapeDtypeStruct(total, jnp.float32),
        scratch_shapes=[
            pltpu.VMEM((3, 2, pieces, rows, cols), jnp.bfloat16),
            pltpu.VMEM((16, sum(widths), cols), jnp.bfloat16),
            pltpu.SemaphoreType.DMA((3, 2)),
            pltpu.SemaphoreType.DMA((len(trains),)),
            pltpu.SemaphoreType.DMA((len(jobs), 2)),
        ]
        + [pltpu.VMEM((2, rows, span), jnp.float32) for span in spans],
        input_output_aliases=aliases,
        compiler_params=pltpu.CompilerParams(vmem_limit_bytes=67043328),
        cost_estimate=pl.CostEstimate(
            flops=2 * rows * work * 4096,
            bytes_accessed=len(places) * 2 * 2**20 + 32 * sum(widths) * cols + rows * work * 4,
            transcendentals=0,
        ),
    )(*operands)


def on_device(train_features, query_features, precond, example_weight, select):
    _, cols = query_features.shape
    where = jnp.stack(
        [lax.axis_index(name) for name in ("y", "xh", "c", "z", "xl")]
    ).astype(jnp.int32)

    pieces = train_features.reshape(16, -1, cols)
    starts = [sum(WIDTHS[:n]) for n in range(len(WIDTHS))]
    cuts = []
    for start, width in zip(starts, WIDTHS):
        cuts.append(pieces[:, start : start + width])

    p = lax.all_to_all(
        split_quarter(where, precond, cols), PB, split_axis=0, concat_axis=0, tiled=True
    )
    p = ring(p, "y")
    q_x = lax.ppermute(query_features, "xl", [(0, 1), (1, 0)])
    q_pair = stack(query_features, q_x)
    q_ring = ring(q_pair, "z")
    q_own = stack(*q_ring)
    q_other = swap(q_own)
    tile = conditioned_tile(where, p, (q_own, q_other))

    plane = lax.all_to_all(tile, ("z", "xl"), split_axis=0, concat_axis=0, tiled=True)
    other = lax.ppermute(plane, ("xh", "xl"), [(0, 3), (1, 2), (2, 1), (3, 0)])
    s1 = shift(plane, 1)
    s3 = shift(plane, -1)
    o1 = shift(other, 1)
    o3 = shift(other, -1)
    s2 = shift(s1, 1)
    o2 = shift(o3, -1)

    def unit(x):
        return [x, swap(x)]

    near = unit(plane) + unit(other) + unit(s1) + unit(s3)
    near += unit(o1) + unit(o3)
    far = unit(s2) + unit(o2)
    near_at = ((0, 0), (0, 1), (3, 0), (1, 0), (3, 1), (1, 1))
    far_at = ((2, 0), (2, 1))
    trains = []
    for cut in cuts:
        trains.append(lax.all_to_all(cut, PB, split_axis=0, concat_axis=0, tiled=True))
    factor = (
        jnp.repeat(select.astype(jnp.float32), BLK, axis=1)
        * (example_weight * (16 * cols) ** (-0.5))[None, :]
    ).reshape(8, 2, -1)
    out = None
    total = (2048, sum(WIDTHS))
    jobs = [(0, 6, 0, 2)]
    out = scores(where, near, near_at, trains[:2], jobs, factor, 0, total, None)
    jobs = [(0, 6, 2, 3), (6, 8, 0, 3)]
    out = scores(where, near + far, near_at + far_at, trains, jobs, factor, 0, total, out)
    return out


def solution(mesh):
    fine = Mesh(mesh.devices.reshape(4, 2, 4, 2, 2), ("y", "xh", "z", "xl", "c"))
    ex, pb, both = ("y", "xh"), PB, ("y", "xh", *PB)
    placed = (P(ex, pb), P(ex, pb), P(pb, None), P(both), P(None, both))

    return jax.shard_map(on_device, mesh=fine, in_specs=placed, out_specs=P(None, both), check_vma=False)
```

time: 384 us -> 220 us (0.57)
  waiting for transfers between devices: 221 us -> 109 us
  blocking collectives: 97.5 us -> 0 us
  starting transfers between devices: 7.52 us -> 58.1 us
  Pallas kernels: 0 us -> 37.6 us
  matrix products: 26.2 us -> 0 us
  between operations: 13.4 us -> 0.32 us
  local copies, waits for them, and re-layouts: 17.3 us -> 13.4 us
    all_to_all x1 -> x5, waiting for transfers between devices: 150 us -> 13.8 us  [the longest x1 10.1 us: on_device(): lax.all_to_all(tile, ('z', 'xl'), split_axis=0, concat_axis=0, tiled=True)]
    psum x1 -> x0, blocking collectives: 97.5 us -> none  [on_device(): lax.psum(jnp.dot(query_features, precond, preferred_element_type=jnp.floa...]
    ppermute x0 -> x23, waiting for transfers between devices: none -> 95.6 us  [the longest x6 33.5 us: ring(): got[by] = lax.ppermute(x, axis, [(i, (i + by) % 4) for i in range(4)])]
    all_gather x1 -> x0, waiting for transfers between devices: 70.8 us -> none  [on_device(): lax.all_gather(gathered, 'ex', axis=0, tiled=True)]
    pallas_call x0 -> x6, Pallas kernels: none -> 37.6 us  [the longest x2 32.6 us: scores(): pl.pallas_call(lambda *refs: score_kernel(places, widths, jobs, first, *r...]
    all_to_all x1 -> x5, starting transfers between devices: 7.52 us -> 33.8 us  [the longest x3 16.6 us: on_device(): lax.all_to_all(cut, PB, split_axis=0, concat_axis=0, tiled=True)]
    dot_general x2 -> x0, matrix products: 26.2 us -> none  [the longest x1 22.6 us: tile_product(): lax.dot_general(portion, train_tile, (((1,), (1,)), ((), ())), preferred_...]
    ppermute x0 -> x23, starting transfers between devices: none -> 24.3 us  [the longest x9 9.56 us: swap(): return lax.ppermute(x, 'c', [(0, 1), (1, 0)])]
  transfers between devices with their start and end apart: 2 -> 28, of which waited for: 2 -> 11; matrix products, arithmetic and copies ran while one was open for 3% -> 5% of each run, Pallas kernels for 0% -> 9%
where the time goes in v2:
time: 220 us; the launch traced here: 219 us
  waiting for transfers between devices  109 us (50%)
  starting transfers between devices  58.1 us (26%)
  Pallas kernels  37.6 us (17%)
  local copies, waits for them, and re-layouts  13.4 us (6%)
    ppermute x6, waiting for transfers between devices, ring(): got[by] = lax.ppermute(x, axis, [(i, (i + by) % 4) for i in range(4)])  33.5 us
    pallas_call x2, Pallas kernels, scores(): pl.pallas_call(lambda *refs: score_kernel(places, widths, jobs, first, *r...  32.6 us
    ppermute x6, waiting for transfers between devices, shift(): return lax.ppermute(x, 'y', [(i, (i + by) % 4) for i in range(4)])  32.1 us
    ppermute x1, waiting for transfers between devices, on_device(): other = lax.ppermute(plane, ('xh', 'xl'), [(0, 3), (1, 2), (2, 1), (3, 0)])  20.4 us
    all_to_all x3, starting transfers between devices, on_device(): lax.all_to_all(cut, PB, split_axis=0, concat_axis=0, tiled=True)  16.6 us
    slice x3, local copies, waits for them, and re-layouts, on_device(): cuts.append(pieces[:, start:start + width])  10.7 us
    all_to_all x1, waiting for transfers between devices, on_device(): lax.all_to_all(tile, ('z', 'xl'), split_axis=0, concat_axis=0, tiled=True)  10.1 us
    ppermute x9, starting transfers between devices, swap(): return lax.ppermute(x, 'c', [(0, 1), (1, 0)])  9.56 us
  transfers between devices with their start and end apart: 28, of which 11 were waited for; matrix products, arithmetic and copies ran while one was open for 5% of the time, Pallas kernels for 9%

profile of v2, /device:TPU:1, one launch (start us, length us, event | category | flops | bytes accessed | tf_op | source)
XLA Modules:
  0.0 219.5 jit_solution(3473903761196621293)
XLA Ops:
  0.0 0.6 stack.23.where.refs_0_
  0.6 2.5 %shard_map.55 = bf16[16,64,256]{2,1,0:T(8,128)(2,1)} custom-call(s32[5]{0:T(128)} %stack.23.where.refs_0_, bf16[256,4096]{1,0:T(8,128)(2,1)} %p.1), custom_call_target="tpu_custom_call" | custom-call | tf_op jit(solution)/shard_map/pallas_call | solution.py:41
  3.1 7.9 %all-to-all-start = ((bf16[16,64,256]{2,1,0:T(8,128)(2,1)}), bf16[16,64,256]{2,1,0:T(8,128)(2,1)S(1)}, u32[]{:S(2)}, u32[]{:S(2)}) async-start(bf16[16,64,256]{2,1,0:T(8,128)(2,1)} %shard_map.55), calls=%async_computation | async-start | bytes 1048576 | tf_op jit(solution)/shard_map/all_to_all | solution.py:257
  11.0 1.4 collective-permute-start.3
  12.4 9.3 %collective-permute-done.3.refs_1_ = bf16[256,256]{1,0:T(8,128)(2,1)S(1)} collective-permute-done((bf16[256,256]{1,0:T(8,128)(2,1)}, bf16[256,256]{1,0:T(8,128)(2,1)S(1)}, u32[]{:S(2)}, u32[]{:S(2)}) %collective-permute-start.3) | collective-permute-done | bytes 131104 | tf_op jit(solution)/shard_map/ppermute | solution.py:261
  21.7 0.9 copy-done
  22.6 2.5 %collective-permute-start.6 = (bf16[2,256,256]{2,1,0:T(8,128)(2,1)S(1)}, bf16[2,256,256]{2,1,0:T(8,128)(2,1)S(1)}, u32[]{:S(2)}, u32[]{:S(2)}) collective-permute-start(bf16[2,256,256]{2,1,0:T(8,128)(2,1)S(1)} %shard_map.56.refs_0_), channel_id=1, source_target_pairs={{0,12},{4,0},{8,4},{12,8},{1,13},{5,1},{9,5},{13,9},{2,14},{6,2},{... | collective-permute-start | bytes 786440 | tf_op jit(solution)/shard_map/ppermute | solution.py:24
  25.1 0.6 collective-permute-start.5
  25.6 0.6 collective-permute-start.4
  26.2 2.5 %slice.12 = bf16[16,160,256]{2,1,0:T(8,128)(2,1)} slice(bf16[16,1024,256]{2,1,0:T(8,128)(2,1)} %bitcast.6), slice={[0:16], [0:160], [0:256]} | slice | bytes 2621440 | tf_op jit(solution)/shard_map/slice | solution.py:255
  28.7 5.5 %all-to-all-start.2 = ((bf16[16,160,256]{2,1,0:T(8,128)(2,1)}), bf16[16,160,256]{2,1,0:T(8,128)(2,1)S(1)}, u32[]{:S(2)}, u32[]{:S(2)}) async-start(bf16[16,160,256]{2,1,0:T(8,128)(2,1)} %slice.12), calls=%async_computation.2 | async-start | bytes 2621440 | tf_op jit(solution)/shard_map/all_to_all | solution.py:287
  34.2 8.0 %collective-permute-done.4.refs_1_ = bf16[2,256,256]{2,1,0:T(8,128)(2,1)S(1)} collective-permute-done((bf16[2,256,256]{2,1,0:T(8,128)(2,1)S(1)}, bf16[2,256,256]{2,1,0:T(8,128)(2,1)S(1)}, u32[]{:S(2)}, u32[]{:S(2)}) %collective-permute-start.4) | collective-permute-done | bytes 262176 | tf_op jit(solution)/shard_map/ppermute | solution.py:24
  42.2 1.8 collective-permute-start.7
  44.1 2.7 %collective-permute-start.2 = (bf16[16,64,256]{2,1,0:T(8,128)(2,1)S(1)}, bf16[16,64,256]{2,1,0:T(8,128)(2,1)S(1)}, u32[]{:S(2)}, u32[]{:S(2)}) collective-permute-start(bf16[16,64,256]{2,1,0:T(8,128)(2,1)S(1)} %all-to-all-done.refs_0_), channel_id=1, source_target_pairs={{0,96},{32,0},{64,32},{96,64},{1,97},{33,1},{65,33},{97,65},{2,98}... | collective-permute-start | bytes 1572872 | tf_op jit(solution)/shard_map/ppermute | solution.py:24
  46.8 0.3 collective-permute-start.1
  47.1 0.7 collective-permute-start
  47.8 21.3 %collective-permute-done.2.refs_3_ = bf16[16,64,256]{2,1,0:T(8,128)(2,1)S(1)} collective-permute-done((bf16[16,64,256]{2,1,0:T(8,128)(2,1)S(1)}, bf16[16,64,256]{2,1,0:T(8,128)(2,1)S(1)}, u32[]{:S(2)}, u32[]{:S(2)}) %collective-permute-start.2) | collective-permute-done | bytes 524320 | tf_op jit(solution)/shard_map/ppermute | solution.py:24
  69.1 4.3 %collective-permute-done.refs_1_ = bf16[16,64,256]{2,1,0:T(8,128)(2,1)S(1)} collective-permute-done((bf16[16,64,256]{2,1,0:T(8,128)(2,1)S(1)}, bf16[16,64,256]{2,1,0:T(8,128)(2,1)S(1)}, u32[]{:S(2)}, u32[]{:S(2)}) %collective-permute-start) | collective-permute-done | bytes 524320 | tf_op jit(solution)/shard_map/ppermute | solution.py:24
  73.4 2.4 %shard_map.58 = bf16[8,256,256]{2,1,0:T(8,128)(2,1)} custom-call(s32[5]{0:T(128)S(1)} %copy-done.1, bf16[16,64,256]{2,1,0:T(8,128)(2,1)S(1)} %all-to-all-done.refs_0_, bf16[16,64,256]{2,1,0:T(8,128)(2,1)S(1)} %collective-permute-done.refs_1_, bf16[16,64,256]{2,1,0:T(8,128)(2,1)S(1)} %collective-permute-done.1.refs_2_, ...), custom_call_target="tpu_custom_call" | custom-call | tf_op jit(solution)/shard_map/pallas_call | solution.py:102
  75.8 9.3 %all-to-all-start.1 = ((bf16[8,256,256]{2,1,0:T(8,128)(2,1)}), bf16[8,256,256]{2,1,0:T(8,128)(2,1)S(1)}, u32[]{:S(2)}, u32[]{:S(2)}) async-start(bf16[8,256,256]{2,1,0:T(8,128)(2,1)} %shard_map.58), calls=%async_computation.1 | async-start | bytes 2097152 | tf_op jit(solution)/shard_map/all_to_all | solution.py:268
  85.1 5.0 %slice.13 = bf16[16,608,256]{2,1,0:T(8,128)(2,1)} slice(bf16[16,1024,256]{2,1,0:T(8,128)(2,1)} %bitcast.7), slice={[0:16], [160:768], [0:256]} | slice | bytes 9961472 | tf_op jit(solution)/shard_map/slice | solution.py:255
  90.1 10.1 %all-to-all-done.1.refs_1_ = bf16[8,256,256]{2,1,0:T(8,128)(2,1)S(1)} async-done(((bf16[8,256,256]{2,1,0:T(8,128)(2,1)}), bf16[8,256,256]{2,1,0:T(8,128)(2,1)S(1)}, u32[]{:S(2)}, u32[]{:S(2)}) %all-to-all-start.1) | async-done | bytes 1048608 | tf_op jit(solution)/shard_map/all_to_all | solution.py:268
  100.2 5.9 %all-to-all-start.3 = ((bf16[16,608,256]{2,1,0:T(8,128)(2,1)}), bf16[16,608,256]{2,1,0:T(8,128)(2,1)}, u32[]{:S(2)}, u32[]{:S(2)}) async-start(bf16[16,608,256]{2,1,0:T(8,128)(2,1)} %slice.13), calls=%async_computation.3 | async-start | bytes 9961472 | tf_op jit(solution)/shard_map/all_to_all | solution.py:287
  106.1 2.7 %collective-permute-start.9 = (bf16[8,256,256]{2,1,0:T(8,128)(2,1)S(1)}, bf16[8,256,256]{2,1,0:T(8,128)(2,1)S(1)}, u32[]{:S(2)}, u32[]{:S(2)}) collective-permute-start(bf16[8,256,256]{2,1,0:T(8,128)(2,1)S(1)} %all-to-all-done.1.refs_1_), channel_id=1, source_target_pairs={{0,18},{2,16},{16,2},{18,0},{1,19},{3,17},{17,3},{19,1},{4,22},{6,... | collective-permute-start | bytes 3145736 | tf_op jit(solution)/shard_map/ppermute | solution.py:269
  108.8 1.5 collective-permute-start.11
  110.3 1.2 collective-permute-start.8
  111.5 20.4 %collective-permute-done.9.refs_3_ = bf16[8,256,256]{2,1,0:T(8,128)(2,1)S(1)} collective-permute-done((bf16[8,256,256]{2,1,0:T(8,128)(2,1)S(1)}, bf16[8,256,256]{2,1,0:T(8,128)(2,1)S(1)}, u32[]{:S(2)}, u32[]{:S(2)}) %collective-permute-start.9) | collective-permute-done | bytes 1048608 | tf_op jit(solution)/shard_map/ppermute | solution.py:269
  132.0 1.0 collective-permute-done.13.refs_7_
  133.0 1.4 collective-permute-start.14
  134.4 0.3 collective-permute-start.19
  134.8 1.8 collective-permute-start.12
  136.5 19.2 %collective-permute-done.17.refs_11_ = bf16[8,256,256]{2,1,0:T(8,128)(2,1)} collective-permute-done((bf16[8,256,256]{2,1,0:T(8,128)(2,1)S(1)}, bf16[8,256,256]{2,1,0:T(8,128)(2,1)}, u32[]{:S(2)}, u32[]{:S(2)}) %collective-permute-start.17) | collective-permute-done | bytes 1048608 | tf_op jit(solution)/shard_map/ppermute | solution.py:18
  155.8 1.5 collective-permute-start.21
  157.2 3.2 %slice.14 = bf16[16,256,256]{2,1,0:T(8,128)(2,1)} slice(bf16[16,1024,256]{2,1,0:T(8,128)(2,1)} %bitcast.8), slice={[0:16], [768:1024], [0:256]} | slice | bytes 4194304 | tf_op jit(solution)/shard_map/slice | solution.py:255
  160.4 3.7 %all-to-all-done.3.refs_14_.refs_18_ = bf16[16,608,256]{2,1,0:T(8,128)(2,1)} async-done(((bf16[16,608,256]{2,1,0:T(8,128)(2,1)}), bf16[16,608,256]{2,1,0:T(8,128)(2,1)}, u32[]{:S(2)}, u32[]{:S(2)}) %all-to-all-start.3) | async-done | bytes 4980768 | tf_op jit(solution)/shard_map/all_to_all | solution.py:287
  164.1 5.1 %all-to-all-start.4 = ((bf16[16,256,256]{2,1,0:T(8,128)(2,1)}), bf16[16,256,256]{2,1,0:T(8,128)(2,1)}, u32[]{:S(2)}, u32[]{:S(2)}) async-start(bf16[16,256,256]{2,1,0:T(8,128)(2,1)} %slice.14), calls=%async_computation.4 | async-start | bytes 4194304 | tf_op jit(solution)/shard_map/all_to_all | solution.py:287
  169.3 0.4 collective-permute-start.10
  169.7 0.2 collective-permute-start.18
  169.9 11.9 %collective-permute-done.15.refs_9_ = bf16[8,256,256]{2,1,0:T(8,128)(2,1)} collective-permute-done((bf16[8,256,256]{2,1,0:T(8,128)(2,1)S(1)}, bf16[8,256,256]{2,1,0:T(8,128)(2,1)}, u32[]{:S(2)}, u32[]{:S(2)}) %collective-permute-start.15) | collective-permute-done | bytes 1048608 | tf_op jit(solution)/shard_map/ppermute | solution.py:18
  181.8 2.2 collective-permute-start.16
  184.1 0.1 broadcast_in_dim.4
  184.2 0.1 collective-permute-start.20
  184.3 0.5 collective-permute-start.22
  184.8 0.6 broadcast_multiply_fusion.refs_15_.refs_20_
  185.5 1.0 copy-done.7
  186.5 0.1 collective-permute-done.16.refs_10_
  186.6 16.9 %shard_map.59.refs_21_ = f32[2048,1024]{1,0:T(8,128)} custom-call(s32[5]{0:T(128)} %stack.23.where.refs_0_, bf16[8,256,256]{2,1,0:T(8,128)(2,1)} %copy-done.3, bf16[8,256,256]{2,1,0:T(8,128)(2,1)} %copy-done.6, bf16[8,256,256]{2,1,0:T(8,128)(2,1)} %copy-done.4, bf16[8,256,256]{2,1,0:T(8,128)(2,1)} %copy-done.7, ...), custom_call_target="tpu_custom_call" | custom-call | flops 9663676416 | bytes 23592960 | tf_op jit(solution)/shard_map/pallas_call | solution.py:222
  203.6 15.7 %shard_map.60 = f32[2048,1024]{1,0:T(8,128)} custom-call(s32[5]{0:T(128)} %stack.23.where.refs_0_, bf16[8,256,256]{2,1,0:T(8,128)(2,1)} %copy-done.3, bf16[8,256,256]{2,1,0:T(8,128)(2,1)} %copy-done.6, bf16[8,256,256]{2,1,0:T(8,128)(2,1)} %copy-done.4, bf16[8,256,256]{2,1,0:T(8,128)(2,1)} %copy-done.7, ...), custom_call_target="tpu_custom_call", output_to_operand_aliasing={{}: (21, {})} | custom-call | flops 7516192768 | bytes 28835840 | tf_op jit(solution)/shard_map/pallas_call | solution.py:222
  (44 shorter events, 0.3 us)
Async XLA Ops:
  3.1 70.2 %copy-start.1 = (s32[5]{0:T(128)S(1)}, s32[5]{0:T(128)}, u32[]{:S(2)}) copy-start(s32[5]{0:T(128)} %stack.23.where.refs_0_) | copy-start | bytes 64
  3.1 25.5 %all-to-all-start = ((bf16[16,64,256]{2,1,0:T(8,128)(2,1)}), bf16[16,64,256]{2,1,0:T(8,128)(2,1)S(1)}, u32[]{:S(2)}, u32[]{:S(2)}) async-start(bf16[16,64,256]{2,1,0:T(8,128)(2,1)} %shard_map.55), calls=%async_computation | async-start | bytes 1048576 | tf_op jit(solution)/shard_map/all_to_all | solution.py:257
  11.0 10.6 %collective-permute-start.3 = (bf16[256,256]{1,0:T(8,128)(2,1)}, bf16[256,256]{1,0:T(8,128)(2,1)S(1)}, u32[]{:S(2)}, u32[]{:S(2)}) collective-permute-start(bf16[256,256]{1,0:T(8,128)(2,1)} %refs_0_.1), channel_id=1, source_target_pairs={{0,2},{2,0},{1,3},{3,1},{4,6},{6,4},{5,7},{7,5},{8,10},{10,8},{9,1... | collective-permute-start | bytes 393224 | tf_op jit(solution)/shard_map/ppermute | solution.py:261
  21.7 0.9 copy-start
  22.6 11.6 %collective-permute-start.6 = (bf16[2,256,256]{2,1,0:T(8,128)(2,1)S(1)}, bf16[2,256,256]{2,1,0:T(8,128)(2,1)S(1)}, u32[]{:S(2)}, u32[]{:S(2)}) collective-permute-start(bf16[2,256,256]{2,1,0:T(8,128)(2,1)S(1)} %shard_map.56.refs_0_), channel_id=1, source_target_pairs={{0,12},{4,0},{8,4},{12,8},{1,13},{5,1},{9,5},{13,9},{2,14},{6,2},{... | collective-permute-start | bytes 786440 | tf_op jit(solution)/shard_map/ppermute | solution.py:24
  25.1 9.1 %collective-permute-start.5 = (bf16[2,256,256]{2,1,0:T(8,128)(2,1)S(1)}, bf16[2,256,256]{2,1,0:T(8,128)(2,1)S(1)}, u32[]{:S(2)}, u32[]{:S(2)}) collective-permute-start(bf16[2,256,256]{2,1,0:T(8,128)(2,1)S(1)} %shard_map.56.refs_0_), channel_id=1, source_target_pairs={{0,8},{4,12},{8,0},{12,4},{1,9},{5,13},{9,1},{13,5},{2,10},{6,14},... | collective-permute-start | bytes 786440 | tf_op jit(solution)/shard_map/ppermute | solution.py:24
  25.6 16.5 %collective-permute-start.4 = (bf16[2,256,256]{2,1,0:T(8,128)(2,1)S(1)}, bf16[2,256,256]{2,1,0:T(8,128)(2,1)S(1)}, u32[]{:S(2)}, u32[]{:S(2)}) collective-permute-start(bf16[2,256,256]{2,1,0:T(8,128)(2,1)S(1)} %shard_map.56.refs_0_), channel_id=1, source_target_pairs={{0,4},{4,8},{8,12},{12,0},{1,5},{5,9},{9,13},{13,1},{2,6},{6,10},{... | collective-permute-start | bytes 786440 | tf_op jit(solution)/shard_map/ppermute | solution.py:24
  28.7 47.1 %all-to-all-start.2 = ((bf16[16,160,256]{2,1,0:T(8,128)(2,1)}), bf16[16,160,256]{2,1,0:T(8,128)(2,1)S(1)}, u32[]{:S(2)}, u32[]{:S(2)}) async-start(bf16[16,160,256]{2,1,0:T(8,128)(2,1)} %slice.12), calls=%async_computation.2 | async-start | bytes 2621440 | tf_op jit(solution)/shard_map/all_to_all | solution.py:287
  42.2 31.1 %collective-permute-start.7 = (bf16[8,256,256]{2,1,0:T(8,128)(2,1)S(1)}, bf16[8,256,256]{2,1,0:T(8,128)(2,1)S(1)}, u32[]{:S(2)}, u32[]{:S(2)}) collective-permute-start(bf16[8,256,256]{2,1,0:T(8,128)(2,1)S(1)} %shard_map.57.refs_4_), channel_id=1, source_target_pairs={{0,1},{1,0},{2,3},{3,2},{4,5},{5,4},{6,7},{7,6},{8,9},{9,8},{10,11... | collective-permute-start | bytes 3145736 | tf_op jit(solution)/shard_map/ppermute | solution.py:29
  44.1 25.0 %collective-permute-start.2 = (bf16[16,64,256]{2,1,0:T(8,128)(2,1)S(1)}, bf16[16,64,256]{2,1,0:T(8,128)(2,1)S(1)}, u32[]{:S(2)}, u32[]{:S(2)}) collective-permute-start(bf16[16,64,256]{2,1,0:T(8,128)(2,1)S(1)} %all-to-all-done.refs_0_), channel_id=1, source_target_pairs={{0,96},{32,0},{64,32},{96,64},{1,97},{33,1},{65,33},{97,65},{2,98}... | collective-permute-start | bytes 1572872 | tf_op jit(solution)/shard_map/ppermute | solution.py:24
  46.8 22.3 %collective-permute-start.1 = (bf16[16,64,256]{2,1,0:T(8,128)(2,1)S(1)}, bf16[16,64,256]{2,1,0:T(8,128)(2,1)S(1)}, u32[]{:S(2)}, u32[]{:S(2)}) collective-permute-start(bf16[16,64,256]{2,1,0:T(8,128)(2,1)S(1)} %all-to-all-done.refs_0_), channel_id=1, source_target_pairs={{0,64},{32,96},{64,0},{96,32},{1,65},{33,97},{65,1},{97,33},{2,66}... | collective-permute-start | bytes 1572872 | tf_op jit(solution)/shard_map/ppermute | solution.py:24
  47.1 26.2 %collective-permute-start = (bf16[16,64,256]{2,1,0:T(8,128)(2,1)S(1)}, bf16[16,64,256]{2,1,0:T(8,128)(2,1)S(1)}, u32[]{:S(2)}, u32[]{:S(2)}) collective-permute-start(bf16[16,64,256]{2,1,0:T(8,128)(2,1)S(1)} %all-to-all-done.refs_0_), channel_id=1, source_target_pairs={{0,32},{32,64},{64,96},{96,0},{1,33},{33,65},{65,97},{97,1},{2,34}... | collective-permute-start | bytes 1572872 | tf_op jit(solution)/shard_map/ppermute | solution.py:24
  75.8 14.3 %copy-start.2 = (bf16[16,160,256]{2,1,0:T(8,128)(2,1)}, bf16[16,160,256]{2,1,0:T(8,128)(2,1)S(1)}, u32[]{:S(2)}) copy-start(bf16[16,160,256]{2,1,0:T(8,128)(2,1)S(1)} %all-to-all-done.2.refs_13_.refs_17_) | copy-start | bytes 3932164
  75.8 24.4 %all-to-all-start.1 = ((bf16[8,256,256]{2,1,0:T(8,128)(2,1)}), bf16[8,256,256]{2,1,0:T(8,128)(2,1)S(1)}, u32[]{:S(2)}, u32[]{:S(2)}) async-start(bf16[8,256,256]{2,1,0:T(8,128)(2,1)} %shard_map.58), calls=%async_computation.1 | async-start | bytes 2097152 | tf_op jit(solution)/shard_map/all_to_all | solution.py:268
  100.2 60.3 %copy-start.3 = (bf16[8,256,256]{2,1,0:T(8,128)(2,1)}, bf16[8,256,256]{2,1,0:T(8,128)(2,1)S(1)}, u32[]{:S(2)}) copy-start(bf16[8,256,256]{2,1,0:T(8,128)(2,1)S(1)} %all-to-all-done.1.refs_1_) | copy-start | bytes 3145732
  100.2 64.0 %all-to-all-start.3 = ((bf16[16,608,256]{2,1,0:T(8,128)(2,1)}), bf16[16,608,256]{2,1,0:T(8,128)(2,1)}, u32[]{:S(2)}, u32[]{:S(2)}) async-start(bf16[16,608,256]{2,1,0:T(8,128)(2,1)} %slice.13), calls=%async_computation.3 | async-start | bytes 9961472 | tf_op jit(solution)/shard_map/all_to_all | solution.py:287
  106.1 77.9 %copy-start.8 = (s32[16,8]{0,1:T(8,128)S(1)}, s32[16,8]{0,1:T(8,128)}, u32[]{:S(2)}) copy-start(s32[16,8]{0,1:T(8,128)} %param.9) | copy-start | bytes 1540
  106.1 78.1 %copy-start.9 = (f32[1024]{0:T(1024)S(1)}, f32[1024]{0:T(1024)}, u32[]{:S(2)}) copy-start(f32[1024]{0:T(1024)} %param.8) | copy-start | bytes 12292
  106.1 25.8 %collective-permute-start.9 = (bf16[8,256,256]{2,1,0:T(8,128)(2,1)S(1)}, bf16[8,256,256]{2,1,0:T(8,128)(2,1)S(1)}, u32[]{:S(2)}, u32[]{:S(2)}) collective-permute-start(bf16[8,256,256]{2,1,0:T(8,128)(2,1)S(1)} %all-to-all-done.1.refs_1_), channel_id=1, source_target_pairs={{0,18},{2,16},{16,2},{18,0},{1,19},{3,17},{17,3},{19,1},{4,22},{6,... | collective-permute-start | bytes 3145736 | tf_op jit(solution)/shard_map/ppermute | solution.py:269
  108.8 24.2 %collective-permute-start.13 = (bf16[8,256,256]{2,1,0:T(8,128)(2,1)S(1)}, bf16[8,256,256]{2,1,0:T(8,128)(2,1)S(1)}, u32[]{:S(2)}, u32[]{:S(2)}) collective-permute-start(bf16[8,256,256]{2,1,0:T(8,128)(2,1)S(1)} %all-to-all-done.1.refs_1_), channel_id=1, source_target_pairs={{0,96},{32,0},{64,32},{96,64},{1,97},{33,1},{65,33},{97,65},{2,98}... | collective-permute-start | bytes 3145736 | tf_op jit(solution)/shard_map/ppermute | solution.py:18
  108.8 25.6 %collective-permute-start.11 = (bf16[8,256,256]{2,1,0:T(8,128)(2,1)S(1)}, bf16[8,256,256]{2,1,0:T(8,128)(2,1)}, u32[]{:S(2)}, u32[]{:S(2)}) collective-permute-start(bf16[8,256,256]{2,1,0:T(8,128)(2,1)S(1)} %all-to-all-done.1.refs_1_), channel_id=1, source_target_pairs={{0,32},{32,64},{64,96},{96,0},{1,33},{33,65},{65,97},{97,1},{2,34}... | collective-permute-start | bytes 3145736 | tf_op jit(solution)/shard_map/ppermute | solution.py:18
  110.3 24.5 %collective-permute-start.8 = (bf16[8,256,256]{2,1,0:T(8,128)(2,1)S(1)}, bf16[8,256,256]{2,1,0:T(8,128)(2,1)S(1)}, u32[]{:S(2)}, u32[]{:S(2)}) collective-permute-start(bf16[8,256,256]{2,1,0:T(8,128)(2,1)S(1)} %all-to-all-done.1.refs_1_), channel_id=1, source_target_pairs={{0,1},{1,0},{2,3},{3,2},{4,5},{5,4},{6,7},{7,6},{8,9},{9,8},{10,11... | collective-permute-start | bytes 3145736 | tf_op jit(solution)/shard_map/ppermute | solution.py:29
  132.0 37.3 %copy-start.4 = (bf16[8,256,256]{2,1,0:T(8,128)(2,1)}, bf16[8,256,256]{2,1,0:T(8,128)(2,1)S(1)}, u32[]{:S(2)}) copy-start(bf16[8,256,256]{2,1,0:T(8,128)(2,1)S(1)} %collective-permute-done.9.refs_3_) | copy-start | bytes 3145732
  132.0 23.8 %collective-permute-start.17 = (bf16[8,256,256]{2,1,0:T(8,128)(2,1)S(1)}, bf16[8,256,256]{2,1,0:T(8,128)(2,1)}, u32[]{:S(2)}, u32[]{:S(2)}) collective-permute-start(bf16[8,256,256]{2,1,0:T(8,128)(2,1)S(1)} %collective-permute-done.9.refs_3_), channel_id=1, source_target_pairs={{0,96},{32,0},{64,32},{96,64},{1,97},{33,1},{65,33},{97,65},{2,98}... | collective-permute-start | bytes 3145736 | tf_op jit(solution)/shard_map/ppermute | solution.py:18
  133.0 52.5 %copy-start.5 = (bf16[8,256,256]{2,1,0:T(8,128)(2,1)}, bf16[8,256,256]{2,1,0:T(8,128)(2,1)S(1)}, u32[]{:S(2)}) copy-start(bf16[8,256,256]{2,1,0:T(8,128)(2,1)S(1)} %collective-permute-done.13.refs_7_) | copy-start | bytes 3145732
  133.0 36.3 %collective-permute-start.14 = (bf16[8,256,256]{2,1,0:T(8,128)(2,1)S(1)}, bf16[8,256,256]{2,1,0:T(8,128)(2,1)}, u32[]{:S(2)}, u32[]{:S(2)}) collective-permute-start(bf16[8,256,256]{2,1,0:T(8,128)(2,1)S(1)} %collective-permute-done.13.refs_7_), channel_id=1, source_target_pairs={{0,1},{1,0},{2,3},{3,2},{4,5},{5,4},{6,7},{7,6},{8,9},{9,8},{10,11... | collective-permute-start | bytes 3145736 | tf_op jit(solution)/shard_map/ppermute | solution.py:29
  134.4 35.3 %collective-permute-start.19 = (bf16[8,256,256]{2,1,0:T(8,128)(2,1)}, bf16[8,256,256]{2,1,0:T(8,128)(2,1)}, u32[]{:S(2)}, u32[]{:S(2)}) collective-permute-start(bf16[8,256,256]{2,1,0:T(8,128)(2,1)} %collective-permute-done.11.refs_5_), channel_id=1, source_target_pairs={{0,32},{32,64},{64,96},{96,0},{1,33},{33,65},{65,97},{97,1},{2,34}... | collective-permute-start | bytes 3145736 | tf_op jit(solution)/shard_map/ppermute | solution.py:18
  134.7 47.1 %collective-permute-start.15 = (bf16[8,256,256]{2,1,0:T(8,128)(2,1)S(1)}, bf16[8,256,256]{2,1,0:T(8,128)(2,1)}, u32[]{:S(2)}, u32[]{:S(2)}) collective-permute-start(bf16[8,256,256]{2,1,0:T(8,128)(2,1)S(1)} %collective-permute-done.9.refs_3_), channel_id=1, source_target_pairs={{0,32},{32,64},{64,96},{96,0},{1,33},{33,65},{65,97},{97,1},{2,34}... | collective-permute-start | bytes 3145736 | tf_op jit(solution)/shard_map/ppermute | solution.py:18
  134.8 21.0 %copy-start.6 = (bf16[8,256,256]{2,1,0:T(8,128)(2,1)}, bf16[8,256,256]{2,1,0:T(8,128)(2,1)S(1)}, u32[]{:S(2)}) copy-start(bf16[8,256,256]{2,1,0:T(8,128)(2,1)S(1)} %collective-permute-done.8.refs_2_) | copy-start | bytes 3145732
  134.8 49.4 %collective-permute-start.12 = (bf16[8,256,256]{2,1,0:T(8,128)(2,1)}, bf16[8,256,256]{2,1,0:T(8,128)(2,1)}, u32[]{:S(2)}, u32[]{:S(2)}) collective-permute-start(bf16[8,256,256]{2,1,0:T(8,128)(2,1)} %collective-permute-done.11.refs_5_), channel_id=1, source_target_pairs={{0,1},{1,0},{2,3},{3,2},{4,5},{5,4},{6,7},{7,6},{8,9},{9,8},{10,11... | collective-permute-start | bytes 3145736 | tf_op jit(solution)/shard_map/ppermute | solution.py:29
  155.8 28.6 %collective-permute-start.21 = (bf16[8,256,256]{2,1,0:T(8,128)(2,1)}, bf16[8,256,256]{2,1,0:T(8,128)(2,1)}, u32[]{:S(2)}, u32[]{:S(2)}) collective-permute-start(bf16[8,256,256]{2,1,0:T(8,128)(2,1)} %collective-permute-done.17.refs_11_), channel_id=1, source_target_pairs={{0,96},{32,0},{64,32},{96,64},{1,97},{33,1},{65,33},{97,65},{2,98}... | collective-permute-start | bytes 3145736 | tf_op jit(solution)/shard_map/ppermute | solution.py:18
  164.1 39.4 %all-to-all-start.4 = ((bf16[16,256,256]{2,1,0:T(8,128)(2,1)}), bf16[16,256,256]{2,1,0:T(8,128)(2,1)}, u32[]{:S(2)}, u32[]{:S(2)}) async-start(bf16[16,256,256]{2,1,0:T(8,128)(2,1)} %slice.14), calls=%async_computation.4 | async-start | bytes 4194304 | tf_op jit(solution)/shard_map/all_to_all | solution.py:287
  169.3 16.2 %collective-permute-start.10 = (bf16[8,256,256]{2,1,0:T(8,128)(2,1)S(1)}, bf16[8,256,256]{2,1,0:T(8,128)(2,1)S(1)}, u32[]{:S(2)}, u32[]{:S(2)}) collective-permute-start(bf16[8,256,256]{2,1,0:T(8,128)(2,1)S(1)} %collective-permute-done.9.refs_3_), channel_id=1, source_target_pairs={{0,1},{1,0},{2,3},{3,2},{4,5},{5,4},{6,7},{7,6},{8,9},{9,8},{10,11... | collective-permute-start | bytes 3145736 | tf_op jit(solution)/shard_map/ppermute | solution.py:29
  169.7 15.8 %collective-permute-start.18 = (bf16[8,256,256]{2,1,0:T(8,128)(2,1)}, bf16[8,256,256]{2,1,0:T(8,128)(2,1)}, u32[]{:S(2)}, u32[]{:S(2)}) collective-permute-start(bf16[8,256,256]{2,1,0:T(8,128)(2,1)} %collective-permute-done.17.refs_11_), channel_id=1, source_target_pairs={{0,1},{1,0},{2,3},{3,2},{4,5},{5,4},{6,7},{7,6},{8,9},{9,8},{10,11... | collective-permute-start | bytes 3145736 | tf_op jit(solution)/shard_map/ppermute | solution.py:29
  181.8 4.8 %collective-permute-start.16 = (bf16[8,256,256]{2,1,0:T(8,128)(2,1)}, bf16[8,256,256]{2,1,0:T(8,128)(2,1)}, u32[]{:S(2)}, u32[]{:S(2)}) collective-permute-start(bf16[8,256,256]{2,1,0:T(8,128)(2,1)} %collective-permute-done.15.refs_9_), channel_id=1, source_target_pairs={{0,1},{1,0},{2,3},{3,2},{4,5},{5,4},{6,7},{7,6},{8,9},{9,8},{10,11... | collective-permute-start | bytes 3145736 | tf_op jit(solution)/shard_map/ppermute | solution.py:29
  184.2 19.4 %collective-permute-start.20 = (bf16[8,256,256]{2,1,0:T(8,128)(2,1)}, bf16[8,256,256]{2,1,0:T(8,128)(2,1)}, u32[]{:S(2)}, u32[]{:S(2)}) collective-permute-start(bf16[8,256,256]{2,1,0:T(8,128)(2,1)} %collective-permute-done.19.refs_13_), channel_id=1, source_target_pairs={{0,1},{1,0},{2,3},{3,2},{4,5},{5,4},{6,7},{7,6},{8,9},{9,8},{10,11... | collective-permute-start | bytes 3145736 | tf_op jit(solution)/shard_map/ppermute | solution.py:29
  184.3 19.3 %collective-permute-start.22 = (bf16[8,256,256]{2,1,0:T(8,128)(2,1)}, bf16[8,256,256]{2,1,0:T(8,128)(2,1)}, u32[]{:S(2)}, u32[]{:S(2)}) collective-permute-start(bf16[8,256,256]{2,1,0:T(8,128)(2,1)} %collective-permute-done.21.refs_15_), channel_id=1, source_target_pairs={{0,1},{1,0},{2,3},{3,2},{4,5},{5,4},{6,7},{7,6},{8,9},{9,8},{10,11... | collective-permute-start | bytes 3145736 | tf_op jit(solution)/shard_map/ppermute | solution.py:29
  185.5 1.0 copy-start.7

commit v3 on v2

--- a/solution.py
+++ b/solution.py
@@ -10,7 +10,6 @@
 WIDTHS = (160, 608, 256)
 
 IN_VMEM = pl.BlockSpec(memory_space=pltpu.VMEM)
-IN_SMEM = pl.BlockSpec(memory_space=pltpu.SMEM)
 ANYWHERE = pl.BlockSpec(memory_space=pl.ANY)
 
 
@@ -29,26 +28,32 @@
     return lax.ppermute(x, "c", [(0, 1), (1, 0)])
 
 
-def split_kernel(where, p, out):
-    cols = out.shape[2]
-    for j in range(out.shape[0]):
-        out[j] = p[:, j * cols : (j + 1) * cols]
-
-
-def split_quarter(where, precond, cols):
+def split_kernel(p, out, sems):
+    blocks, rows, cols = out.shape
+    start = pl.multiple_of(lax.axis_index("y") * rows, rows)
+    copies = [
+        pltpu.make_async_copy(
+            p.at[pl.ds(start, rows), pl.ds(j * cols, cols)], out.at[j], sems.at[j]
+        )
+        for j in range(blocks)
+    ]
+    for copy in copies:
+        copy.start()
+    for copy in copies:
+        copy.wait()
+
+
+def split_quarter(precond, cols):
     rows = precond.shape[0] // 4
     blocks = precond.shape[1] // cols
     return pl.pallas_call(
         split_kernel,
-        grid_spec=pltpu.PrefetchScalarGridSpec(
-            num_scalar_prefetch=1,
-            grid=(1,),
-            in_specs=[pl.BlockSpec((rows, precond.shape[1]), lambda i, where: (where[0], 0))],
-            out_specs=pl.BlockSpec((blocks, rows, cols), lambda i, where: (0, 0, 0)),
-        ),
+        in_specs=[ANYWHERE],
+        out_specs=IN_VMEM,
         out_shape=jax.ShapeDtypeStruct((blocks, rows, cols), precond.dtype),
+        scratch_shapes=[pltpu.SemaphoreType.DMA((blocks,))],
         compiler_params=pltpu.CompilerParams(vmem_limit_bytes=60 * 2**20),
-    )(where, precond)
+    )(precond)
 
 
 def stack_kernel(*refs):
@@ -74,9 +79,9 @@
     )(*parts)
 
 
-def tile_kernel(where, *refs):
+def tile_kernel(*refs):
     p, q, (out, whole) = refs[:4], refs[4:-2], refs[-2:]
-    y, core, z, xl = where[0], where[2], where[3], where[4]
+    y, core, z, xl = (lax.axis_index(name) for name in ("y", "c", "z", "xl"))
     quarter = p[0].shape[1]
     for back in range(4):
         start = pl.multiple_of(lax.rem(y + 4 - back, 4) * quarter, quarter)
@@ -97,24 +102,24 @@
         out[k] = tile
 
 
-def conditioned_tile(where, p, q):
+def conditioned_tile(p, q):
     rows = q[0].shape[1]
     return pl.pallas_call(
         tile_kernel,
-        in_specs=[IN_SMEM] + [IN_VMEM] * (len(p) + len(q)),
+        in_specs=[IN_VMEM] * (len(p) + len(q)),
         out_specs=IN_VMEM,
         out_shape=jax.ShapeDtypeStruct((8, rows, rows), jnp.bfloat16),
         scratch_shapes=[pltpu.VMEM((16, rows, rows), jnp.bfloat16)],
         compiler_params=pltpu.CompilerParams(vmem_limit_bytes=12 * 2**20),
-    )(where, *p, *q)
-
-
-def score_kernel(places, widths, jobs, first, where, *refs):
+    )(*p, *q)
+
+
+def score_kernel(places, widths, jobs, first, *refs):
     n, m = len(places), len(widths)
     units, trains, factor = refs[: 2 * n], refs[2 * n : 2 * n + m], refs[2 * n + m]
     held, rows_t, unit_sem, train_sem, out_sem = refs[-5 - len(jobs) : -len(jobs)]
     out, readies = refs[-6 - len(jobs)], refs[-len(jobs) :]
-    y, xh, core = where[0], where[1], where[2]
+    y, xh, core = (lax.axis_index(name) for name in ("y", "xh", "c"))
     slots, rows = held.shape[0], held.shape[3]
     at = [sum(widths[:k]) for k in range(m + 1)]
 
@@ -207,11 +212,11 @@
             ).wait()
 
 
-def scores(where, units, places, trains, jobs, factor, first, total, previous):
+def scores(units, places, trains, jobs, factor, first, total, previous):
     widths = [train.shape[1] for train in trains]
     pieces, rows, cols = units[0].shape
-    operands = [where, *units, *trains, factor]
-    specs = [IN_SMEM] + [ANYWHERE] * (len(units) + len(trains)) + [IN_VMEM]
+    operands = [*units, *trains, factor]
+    specs = [ANYWHERE] * (len(units) + len(trains)) + [IN_VMEM]
     aliases = {}
     if previous is not None:
         aliases = {len(operands): 0}
@@ -244,26 +249,20 @@
 
 def on_device(train_features, query_features, precond, example_weight, select):
     _, cols = query_features.shape
-    where = jnp.stack(
-        [lax.axis_index(name) for name in ("y", "xh", "c", "z", "xl")]
-    ).astype(jnp.int32)
-
     pieces = train_features.reshape(16, -1, cols)
     starts = [sum(WIDTHS[:n]) for n in range(len(WIDTHS))]
     cuts = []
     for start, width in zip(starts, WIDTHS):
         cuts.append(pieces[:, start : start + width])
 
-    p = lax.all_to_all(
-        split_quarter(where, precond, cols), PB, split_axis=0, concat_axis=0, tiled=True
-    )
+    p = lax.all_to_all(split_quarter(precond, cols), PB, split_axis=0, concat_axis=0, tiled=True)
     p = ring(p, "y")
     q_x = lax.ppermute(query_features, "xl", [(0, 1), (1, 0)])
     q_pair = stack(query_features, q_x)
     q_ring = ring(q_pair, "z")
     q_own = stack(*q_ring)
     q_other = swap(q_own)
-    tile = conditioned_tile(where, p, (q_own, q_other))
+    tile = conditioned_tile(p, (q_own, q_other))
 
     plane = lax.all_to_all(tile, ("z", "xl"), split_axis=0, concat_axis=0, tiled=True)
     other = lax.ppermute(plane, ("xh", "xl"), [(0, 3), (1, 2), (2, 1), (3, 0)])
@@ -292,9 +291,12 @@
     out = None
     total = (2048, sum(WIDTHS))
     jobs = [(0, 6, 0, 2)]
-    out = scores(where, near, near_at, trains[:2], jobs, factor, 0, total, None)
-    jobs = [(0, 6, 2, 3), (6, 8, 0, 3)]
-    out = scores(where, near + far, near_at + far_at, trains, jobs, factor, 0, total, out)
+    out = scores(near, near_at, trains[:2], jobs, factor, 0, total, None)
+    jobs = [(0, 2, 0, 2)]
+    out = scores(far, far_at, trains[:2], jobs, factor, 0, total, out)
+    jobs = [(0, 8, 0, 1)]
+    units, places = near + far, near_at + far_at
+    out = scores(units, places, trains[2:], jobs, factor, starts[2], total, out)
     return out
 
 

time: 220 us -> 212 us (0.964)
  waiting for transfers between devices: 109 us -> 89.2 us
  starting transfers between devices: 58.1 us -> 66.5 us
  Pallas kernels: 37.6 us -> 41 us
    ppermute x6, waiting for transfers between devices: 33.5 us -> 24.2 us  [ring(): got[by] = lax.ppermute(x, axis, [(i, (i + by) % 4) for i in range(4)])]
    ppermute x6, starting transfers between devices: 3.31 us -> 9.38 us  [shift(): return lax.ppermute(x, 'y', [(i, (i + by) % 4) for i in range(4)])]
    ppermute x6, waiting for transfers between devices: 32.1 us -> 27.2 us  [shift(): return lax.ppermute(x, 'y', [(i, (i + by) % 4) for i in range(4)])]
    pallas_call x2 -> x3, Pallas kernels: 32.6 us -> 37.1 us  [scores(): pl.pallas_call(lambda *refs: score_kernel(places, widths, jobs, first, *r...]
    all_to_all x3, waiting for transfers between devices: 3.7 us -> 0.01 us  [on_device(): lax.all_to_all(cut, PB, split_axis=0, concat_axis=0, tiled=True)]
    ppermute x6, starting transfers between devices: 7.4 us -> 9.8 us  [ring(): got[by] = lax.ppermute(x, axis, [(i, (i + by) % 4) for i in range(4)])]
  transfers between devices with their start and end apart: 28 -> 28, of which waited for: 11 -> 8; matrix products, arithmetic and copies ran while one was open for 5% -> 5% of each run, Pallas kernels for 9% -> 13%
where the time goes in v3:
time: 212 us; the launch traced here: 211 us
  waiting for transfers between devices  89.2 us (42%)
  starting transfers between devices  66.5 us (31%)
  Pallas kernels  41 us (19%)
  local copies, waits for them, and re-layouts  13.6 us (6%)
    pallas_call x3, Pallas kernels, scores(): pl.pallas_call(lambda *refs: score_kernel(places, widths, jobs, first, *r...  37.1 us
    ppermute x6, waiting for transfers between devices, shift(): return lax.ppermute(x, 'y', [(i, (i + by) % 4) for i in range(4)])  27.2 us
    ppermute x6, waiting for transfers between devices, ring(): got[by] = lax.ppermute(x, axis, [(i, (i + by) % 4) for i in range(4)])  24.2 us
    ppermute x1, waiting for transfers between devices, on_device(): other = lax.ppermute(plane, ('xh', 'xl'), [(0, 3), (1, 2), (2, 1), (3, 0)])  19.2 us
    all_to_all x3, starting transfers between devices, on_device(): lax.all_to_all(cut, PB, split_axis=0, concat_axis=0, tiled=True)  17 us
    ppermute x9, starting transfers between devices, swap(): return lax.ppermute(x, 'c', [(0, 1), (1, 0)])  10.9 us
    slice x3, local copies, waits for them, and re-layouts, on_device(): cuts.append(pieces[:, start:start + width])  10.7 us
    ppermute x6, starting transfers between devices, ring(): got[by] = lax.ppermute(x, axis, [(i, (i + by) % 4) for i in range(4)])  9.8 us
  transfers between devices with their start and end apart: 28, of which 8 were waited for; matrix products, arithmetic and copies ran while one was open for 5% of the time, Pallas kernels for 13%

profile of v3, /device:TPU:1, one launch (start us, length us, event | category | flops | bytes accessed | tf_op | source)
XLA Modules:
  0.0 211.3 jit_solution(1688998076903317436)
XLA Ops:
  0.0 1.9 shard_map.55
  1.9 7.8 %all-to-all-start = ((bf16[16,64,256]{2,1,0:T(8,128)(2,1)}), bf16[16,64,256]{2,1,0:T(8,128)(2,1)S(1)}, u32[]{:S(2)}, u32[]{:S(2)}) async-start(bf16[16,64,256]{2,1,0:T(8,128)(2,1)} %shard_map.55), calls=%async_computation | async-start | bytes 1048576 | tf_op jit(solution)/shard_map/all_to_all | solution.py:258
  9.7 1.4 collective-permute-start.3
  11.1 9.3 %collective-permute-done.3.refs_1_ = bf16[256,256]{1,0:T(8,128)(2,1)S(1)} collective-permute-done((bf16[256,256]{1,0:T(8,128)(2,1)}, bf16[256,256]{1,0:T(8,128)(2,1)S(1)}, u32[]{:S(2)}, u32[]{:S(2)}) %collective-permute-start.3) | collective-permute-done | bytes 131104 | tf_op jit(solution)/shard_map/ppermute | solution.py:260
  20.4 0.9 copy-done
  21.3 1.3 collective-permute-start.4
  22.5 2.4 %collective-permute-start.5 = (bf16[2,256,256]{2,1,0:T(8,128)(2,1)S(1)}, bf16[2,256,256]{2,1,0:T(8,128)(2,1)S(1)}, u32[]{:S(2)}, u32[]{:S(2)}) collective-permute-start(bf16[2,256,256]{2,1,0:T(8,128)(2,1)S(1)} %shard_map.56.refs_0_), channel_id=1, source_target_pairs={{0,8},{4,12},{8,0},{12,4},{1,9},{5,13},{9,1},{13,5},{2,10},{6,14},... | collective-permute-start | bytes 786440 | tf_op jit(solution)/shard_map/ppermute | solution.py:23
  24.9 1.2 collective-permute-start.6
  26.1 2.5 %slice.13 = bf16[16,160,256]{2,1,0:T(8,128)(2,1)} slice(bf16[16,1024,256]{2,1,0:T(8,128)(2,1)} %bitcast.1), slice={[0:16], [0:160], [0:256]} | slice | bytes 2621440 | tf_op jit(solution)/shard_map/slice | solution.py:256
  28.6 5.3 %all-to-all-start.3 = ((bf16[16,160,256]{2,1,0:T(8,128)(2,1)}), bf16[16,160,256]{2,1,0:T(8,128)(2,1)S(1)}, u32[]{:S(2)}, u32[]{:S(2)}) async-start(bf16[16,160,256]{2,1,0:T(8,128)(2,1)} %slice.13), calls=%async_computation.3 | async-start | bytes 2621440 | tf_op jit(solution)/shard_map/all_to_all | solution.py:286
  33.9 2.1 collective-permute-done.5.refs_2_
  36.1 2.0 collective-permute-start.7
  38.1 1.3 collective-permute-start
  39.4 2.6 %collective-permute-start.1 = (bf16[16,64,256]{2,1,0:T(8,128)(2,1)S(1)}, bf16[16,64,256]{2,1,0:T(8,128)(2,1)S(1)}, u32[]{:S(2)}, u32[]{:S(2)}) collective-permute-start(bf16[16,64,256]{2,1,0:T(8,128)(2,1)S(1)} %all-to-all-done.refs_0_), channel_id=1, source_target_pairs={{0,64},{32,96},{64,0},{96,32},{1,65},{33,97},{65,1},{97,33},{2,66}... | collective-permute-start | bytes 1572872 | tf_op jit(solution)/shard_map/ppermute | solution.py:23
  42.0 1.1 collective-permute-start.2
  43.1 9.7 %collective-permute-done.refs_1_ = bf16[16,64,256]{2,1,0:T(8,128)(2,1)S(1)} collective-permute-done((bf16[16,64,256]{2,1,0:T(8,128)(2,1)S(1)}, bf16[16,64,256]{2,1,0:T(8,128)(2,1)S(1)}, u32[]{:S(2)}, u32[]{:S(2)}) %collective-permute-start) | collective-permute-done | bytes 524320 | tf_op jit(solution)/shard_map/ppermute | solution.py:23
  52.8 12.4 %collective-permute-done.1.refs_2_ = bf16[16,64,256]{2,1,0:T(8,128)(2,1)S(1)} collective-permute-done((bf16[16,64,256]{2,1,0:T(8,128)(2,1)S(1)}, bf16[16,64,256]{2,1,0:T(8,128)(2,1)S(1)}, u32[]{:S(2)}, u32[]{:S(2)}) %collective-permute-start.1) | collective-permute-done | bytes 524320 | tf_op jit(solution)/shard_map/ppermute | solution.py:23
  65.2 1.9 shard_map.58
  67.0 7.5 %all-to-all-start.1 = ((bf16[8,256,256]{2,1,0:T(8,128)(2,1)}), bf16[8,256,256]{2,1,0:T(8,128)(2,1)S(1)}, u32[]{:S(2)}, u32[]{:S(2)}) async-start(bf16[8,256,256]{2,1,0:T(8,128)(2,1)} %shard_map.58), calls=%async_computation.1 | async-start | bytes 2097152 | tf_op jit(solution)/shard_map/all_to_all | solution.py:267
  74.6 5.0 %slice.14 = bf16[16,608,256]{2,1,0:T(8,128)(2,1)} slice(bf16[16,1024,256]{2,1,0:T(8,128)(2,1)} %bitcast.2), slice={[0:16], [160:768], [0:256]} | slice | bytes 9961472 | tf_op jit(solution)/shard_map/slice | solution.py:256
  79.6 9.3 %all-to-all-done.1.refs_0_ = bf16[8,256,256]{2,1,0:T(8,128)(2,1)S(1)} async-done(((bf16[8,256,256]{2,1,0:T(8,128)(2,1)}), bf16[8,256,256]{2,1,0:T(8,128)(2,1)S(1)}, u32[]{:S(2)}, u32[]{:S(2)}) %all-to-all-start.1) | async-done | bytes 1048608 | tf_op jit(solution)/shard_map/all_to_all | solution.py:267
  88.8 6.7 %all-to-all-start.4 = ((bf16[16,608,256]{2,1,0:T(8,128)(2,1)}), bf16[16,608,256]{2,1,0:T(8,128)(2,1)}, u32[]{:S(2)}, u32[]{:S(2)}) async-start(bf16[16,608,256]{2,1,0:T(8,128)(2,1)} %slice.14), calls=%async_computation.4 | async-start | bytes 9961472 | tf_op jit(solution)/shard_map/all_to_all | solution.py:286
  95.6 2.7 %collective-permute-start.9 = (bf16[8,256,256]{2,1,0:T(8,128)(2,1)S(1)}, bf16[8,256,256]{2,1,0:T(8,128)(2,1)S(1)}, u32[]{:S(2)}, u32[]{:S(2)}) collective-permute-start(bf16[8,256,256]{2,1,0:T(8,128)(2,1)S(1)} %all-to-all-done.1.refs_0_), channel_id=1, source_target_pairs={{0,18},{2,16},{16,2},{18,0},{1,19},{3,17},{17,3},{19,1},{4,22},{6,... | collective-permute-start | bytes 3145736 | tf_op jit(solution)/shard_map/ppermute | solution.py:268
  98.3 0.5 collective-permute-start.11
  98.8 2.2 %collective-permute-start.13 = (bf16[8,256,256]{2,1,0:T(8,128)(2,1)S(1)}, bf16[8,256,256]{2,1,0:T(8,128)(2,1)S(1)}, u32[]{:S(2)}, u32[]{:S(2)}) collective-permute-start(bf16[8,256,256]{2,1,0:T(8,128)(2,1)S(1)} %all-to-all-done.1.refs_0_), channel_id=1, source_target_pairs={{0,96},{32,0},{64,32},{96,64},{1,97},{33,1},{65,33},{97,65},{2,98}... | collective-permute-start | bytes 3145736 | tf_op jit(solution)/shard_map/ppermute | solution.py:17
  100.9 1.2 collective-permute-start.8
  102.2 19.2 %collective-permute-done.9.refs_2_ = bf16[8,256,256]{2,1,0:T(8,128)(2,1)S(1)} collective-permute-done((bf16[8,256,256]{2,1,0:T(8,128)(2,1)S(1)}, bf16[8,256,256]{2,1,0:T(8,128)(2,1)S(1)}, u32[]{:S(2)}, u32[]{:S(2)}) %collective-permute-start.9) | collective-permute-done | bytes 1048608 | tf_op jit(solution)/shard_map/ppermute | solution.py:268
  121.4 2.3 %collective-permute-start.17 = (bf16[8,256,256]{2,1,0:T(8,128)(2,1)S(1)}, bf16[8,256,256]{2,1,0:T(8,128)(2,1)}, u32[]{:S(2)}, u32[]{:S(2)}) collective-permute-start(bf16[8,256,256]{2,1,0:T(8,128)(2,1)S(1)} %collective-permute-done.9.refs_2_), channel_id=1, source_target_pairs={{0,96},{32,0},{64,32},{96,64},{1,97},{33,1},{65,33},{97,65},{2,98}... | collective-permute-start | bytes 3145736 | tf_op jit(solution)/shard_map/ppermute | solution.py:17
  123.7 1.4 collective-permute-start.10
  125.1 0.1 collective-permute-start.12
  125.2 0.9 collective-permute-start.19
  126.1 19.1 %collective-permute-done.17.refs_10_ = bf16[8,256,256]{2,1,0:T(8,128)(2,1)} collective-permute-done((bf16[8,256,256]{2,1,0:T(8,128)(2,1)S(1)}, bf16[8,256,256]{2,1,0:T(8,128)(2,1)}, u32[]{:S(2)}, u32[]{:S(2)}) %collective-permute-start.17) | collective-permute-done | bytes 1048608 | tf_op jit(solution)/shard_map/ppermute | solution.py:17
  145.2 3.5 %collective-permute-start.21 = (bf16[8,256,256]{2,1,0:T(8,128)(2,1)}, bf16[8,256,256]{2,1,0:T(8,128)(2,1)}, u32[]{:S(2)}, u32[]{:S(2)}) collective-permute-start(bf16[8,256,256]{2,1,0:T(8,128)(2,1)} %collective-permute-done.17.refs_10_), channel_id=1, source_target_pairs={{0,96},{32,0},{64,32},{96,64},{1,97},{33,1},{65,33},{97,65},{2,98}... | collective-permute-start | bytes 3145736 | tf_op jit(solution)/shard_map/ppermute | solution.py:17
  148.7 3.6 %collective-permute-start.14 = (bf16[8,256,256]{2,1,0:T(8,128)(2,1)S(1)}, bf16[8,256,256]{2,1,0:T(8,128)(2,1)}, u32[]{:S(2)}, u32[]{:S(2)}) collective-permute-start(bf16[8,256,256]{2,1,0:T(8,128)(2,1)S(1)} %collective-permute-done.13.refs_6_), channel_id=1, source_target_pairs={{0,1},{1,0},{2,3},{3,2},{4,5},{5,4},{6,7},{7,6},{8,9},{9,8},{10,11... | collective-permute-start | bytes 3145736 | tf_op jit(solution)/shard_map/ppermute | solution.py:28
  152.3 0.1 collective-permute-start.18
  152.4 0.9 copy-done.7
  153.3 1.0 copy-done.8
  154.3 3.2 %slice.12 = bf16[16,256,256]{2,1,0:T(8,128)(2,1)} slice(bf16[16,1024,256]{2,1,0:T(8,128)(2,1)} %bitcast.3), slice={[0:16], [768:1024], [0:256]} | slice | bytes 4194304 | tf_op jit(solution)/shard_map/slice | solution.py:256
  157.5 5.0 %all-to-all-start.2 = ((bf16[16,256,256]{2,1,0:T(8,128)(2,1)}), bf16[16,256,256]{2,1,0:T(8,128)(2,1)}, u32[]{:S(2)}, u32[]{:S(2)}) async-start(bf16[16,256,256]{2,1,0:T(8,128)(2,1)} %slice.12), calls=%async_computation.2 | async-start | bytes 4194304 | tf_op jit(solution)/shard_map/all_to_all | solution.py:286
  162.5 0.1 copy.8
  162.6 0.1 broadcast_in_dim.4
  162.7 8.1 %collective-permute-done.19.refs_0_.refs_12_ = bf16[8,256,256]{2,1,0:T(8,128)(2,1)} collective-permute-done((bf16[8,256,256]{2,1,0:T(8,128)(2,1)S(1)}, bf16[8,256,256]{2,1,0:T(8,128)(2,1)}, u32[]{:S(2)}, u32[]{:S(2)}) %collective-permute-start.19) | collective-permute-done | bytes 1048608 | tf_op jit(solution)/shard_map/ppermute | solution.py:17
  170.9 2.2 %collective-permute-start.20 = (bf16[8,256,256]{2,1,0:T(8,128)(2,1)}, bf16[8,256,256]{2,1,0:T(8,128)(2,1)}, u32[]{:S(2)}, u32[]{:S(2)}) collective-permute-start(bf16[8,256,256]{2,1,0:T(8,128)(2,1)} %collective-permute-done.19.refs_0_.refs_12_), channel_id=1, source_target_pairs={{0,1},{1,0},{2,3},{3,2},{4,5},{5,4},{6,7},{7,6},{8,9},{9,8},{10,11... | collective-permute-start | bytes 3145736 | tf_op jit(solution)/shard_map/ppermute | solution.py:28
  173.0 0.3 collective-permute-start.22
  173.3 0.6 broadcast_multiply_fusion.refs_14_.refs_6_.refs_17_
  174.0 16.9 %shard_map.59.refs_7_ = f32[2048,1024]{1,0:T(8,128)} custom-call(bf16[8,256,256]{2,1,0:T(8,128)(2,1)} %copy-done.2, bf16[8,256,256]{2,1,0:T(8,128)(2,1)} %copy-done.6, bf16[8,256,256]{2,1,0:T(8,128)(2,1)} %copy-done.3, bf16[8,256,256]{2,1,0:T(8,128)(2,1)} %copy-done.7, bf16[8,256,256]{2,1,0:T(8,128)(2,1)} %copy-done.4, bf16[8,256,256]{2,1,0:T(8,128)(2,1)} %copy-done.8, ...), custom_call_target="tpu_custom_call" | custom-call | flops 9663676416 | bytes 23592960 | tf_op jit(solution)/shard_map/pallas_call | solution.py:227
  190.9 9.4 %shard_map.60.refs_18_ = f32[2048,1024]{1,0:T(8,128)} custom-call(bf16[8,256,256]{2,1,0:T(8,128)(2,1)} %collective-permute-done.19.refs_0_.refs_12_, bf16[8,256,256]{2,1,0:T(8,128)(2,1)} %collective-permute-done.20.refs_1_.refs_13_, bf16[8,256,256]{2,1,0:T(8,128)(2,1)} %collective-permute-done.21.refs_2_.refs_14_, ...), custom_call_target="tpu_custom_call", output_to_operand_aliasing={{}: (7, {})} | custom-call | flops 3221225472 | bytes 12058624 | tf_op jit(solution)/shard_map/pallas_call | solution.py:227
  200.3 10.9 %shard_map.61 = f32[2048,1024]{1,0:T(8,128)} custom-call(bf16[8,256,256]{2,1,0:T(8,128)(2,1)} %copy-done.2, bf16[8,256,256]{2,1,0:T(8,128)(2,1)} %copy-done.6, bf16[8,256,256]{2,1,0:T(8,128)(2,1)} %copy-done.3, bf16[8,256,256]{2,1,0:T(8,128)(2,1)} %copy-done.7, bf16[8,256,256]{2,1,0:T(8,128)(2,1)} %copy-done.4, ...), custom_call_target="tpu_custom_call", output_to_operand_aliasing={{}: (18, {})} | custom-call | flops 4294967296 | bytes 20971520 | tf_op jit(solution)/shard_map/pallas_call | solution.py:227
  (46 shorter events, 0.2 us)
Async XLA Ops:
  1.9 26.6 %all-to-all-start = ((bf16[16,64,256]{2,1,0:T(8,128)(2,1)}), bf16[16,64,256]{2,1,0:T(8,128)(2,1)S(1)}, u32[]{:S(2)}, u32[]{:S(2)}) async-start(bf16[16,64,256]{2,1,0:T(8,128)(2,1)} %shard_map.55), calls=%async_computation | async-start | bytes 1048576 | tf_op jit(solution)/shard_map/all_to_all | solution.py:258
  9.7 10.6 %collective-permute-start.3 = (bf16[256,256]{1,0:T(8,128)(2,1)}, bf16[256,256]{1,0:T(8,128)(2,1)S(1)}, u32[]{:S(2)}, u32[]{:S(2)}) collective-permute-start(bf16[256,256]{1,0:T(8,128)(2,1)} %refs_0_.1), channel_id=1, source_target_pairs={{0,2},{2,0},{1,3},{3,1},{4,6},{6,4},{5,7},{7,5},{8,10},{10,8},{9,1... | collective-permute-start | bytes 393224 | tf_op jit(solution)/shard_map/ppermute | solution.py:260
  20.4 0.9 copy-start
  21.3 12.6 %collective-permute-start.4 = (bf16[2,256,256]{2,1,0:T(8,128)(2,1)S(1)}, bf16[2,256,256]{2,1,0:T(8,128)(2,1)S(1)}, u32[]{:S(2)}, u32[]{:S(2)}) collective-permute-start(bf16[2,256,256]{2,1,0:T(8,128)(2,1)S(1)} %shard_map.56.refs_0_), channel_id=1, source_target_pairs={{0,4},{4,8},{8,12},{12,0},{1,5},{5,9},{9,13},{13,1},{2,6},{6,10},{... | collective-permute-start | bytes 786440 | tf_op jit(solution)/shard_map/ppermute | solution.py:23
  22.5 13.4 %collective-permute-start.5 = (bf16[2,256,256]{2,1,0:T(8,128)(2,1)S(1)}, bf16[2,256,256]{2,1,0:T(8,128)(2,1)S(1)}, u32[]{:S(2)}, u32[]{:S(2)}) collective-permute-start(bf16[2,256,256]{2,1,0:T(8,128)(2,1)S(1)} %shard_map.56.refs_0_), channel_id=1, source_target_pairs={{0,8},{4,12},{8,0},{12,4},{1,9},{5,13},{9,1},{13,5},{2,10},{6,14},... | collective-permute-start | bytes 786440 | tf_op jit(solution)/shard_map/ppermute | solution.py:23
  24.9 11.0 %collective-permute-start.6 = (bf16[2,256,256]{2,1,0:T(8,128)(2,1)S(1)}, bf16[2,256,256]{2,1,0:T(8,128)(2,1)S(1)}, u32[]{:S(2)}, u32[]{:S(2)}) collective-permute-start(bf16[2,256,256]{2,1,0:T(8,128)(2,1)S(1)} %shard_map.56.refs_0_), channel_id=1, source_target_pairs={{0,12},{4,0},{8,4},{12,8},{1,13},{5,1},{9,5},{13,9},{2,14},{6,2},{... | collective-permute-start | bytes 786440 | tf_op jit(solution)/shard_map/ppermute | solution.py:23
  28.6 38.4 %all-to-all-start.3 = ((bf16[16,160,256]{2,1,0:T(8,128)(2,1)}), bf16[16,160,256]{2,1,0:T(8,128)(2,1)S(1)}, u32[]{:S(2)}, u32[]{:S(2)}) async-start(bf16[16,160,256]{2,1,0:T(8,128)(2,1)} %slice.13), calls=%async_computation.3 | async-start | bytes 2621440 | tf_op jit(solution)/shard_map/all_to_all | solution.py:286
  36.1 29.1 %collective-permute-start.7 = (bf16[8,256,256]{2,1,0:T(8,128)(2,1)S(1)}, bf16[8,256,256]{2,1,0:T(8,128)(2,1)S(1)}, u32[]{:S(2)}, u32[]{:S(2)}) collective-permute-start(bf16[8,256,256]{2,1,0:T(8,128)(2,1)S(1)} %shard_map.57.refs_4_), channel_id=1, source_target_pairs={{0,1},{1,0},{2,3},{3,2},{4,5},{5,4},{6,7},{7,6},{8,9},{9,8},{10,11... | collective-permute-start | bytes 3145736 | tf_op jit(solution)/shard_map/ppermute | solution.py:28
  38.1 14.7 %collective-permute-start = (bf16[16,64,256]{2,1,0:T(8,128)(2,1)S(1)}, bf16[16,64,256]{2,1,0:T(8,128)(2,1)S(1)}, u32[]{:S(2)}, u32[]{:S(2)}) collective-permute-start(bf16[16,64,256]{2,1,0:T(8,128)(2,1)S(1)} %all-to-all-done.refs_0_), channel_id=1, source_target_pairs={{0,32},{32,64},{64,96},{96,0},{1,33},{33,65},{65,97},{97,1},{2,34}... | collective-permute-start | bytes 1572872 | tf_op jit(solution)/shard_map/ppermute | solution.py:23
  39.4 25.8 %collective-permute-start.1 = (bf16[16,64,256]{2,1,0:T(8,128)(2,1)S(1)}, bf16[16,64,256]{2,1,0:T(8,128)(2,1)S(1)}, u32[]{:S(2)}, u32[]{:S(2)}) collective-permute-start(bf16[16,64,256]{2,1,0:T(8,128)(2,1)S(1)} %all-to-all-done.refs_0_), channel_id=1, source_target_pairs={{0,64},{32,96},{64,0},{96,32},{1,65},{33,97},{65,1},{97,33},{2,66}... | collective-permute-start | bytes 1572872 | tf_op jit(solution)/shard_map/ppermute | solution.py:23
  42.0 23.2 %collective-permute-start.2 = (bf16[16,64,256]{2,1,0:T(8,128)(2,1)S(1)}, bf16[16,64,256]{2,1,0:T(8,128)(2,1)S(1)}, u32[]{:S(2)}, u32[]{:S(2)}) collective-permute-start(bf16[16,64,256]{2,1,0:T(8,128)(2,1)S(1)} %all-to-all-done.refs_0_), channel_id=1, source_target_pairs={{0,96},{32,0},{64,32},{96,64},{1,97},{33,1},{65,33},{97,65},{2,98}... | collective-permute-start | bytes 1572872 | tf_op jit(solution)/shard_map/ppermute | solution.py:23
  67.0 12.5 %copy-start.1 = (bf16[16,160,256]{2,1,0:T(8,128)(2,1)}, bf16[16,160,256]{2,1,0:T(8,128)(2,1)S(1)}, u32[]{:S(2)}) copy-start(bf16[16,160,256]{2,1,0:T(8,128)(2,1)S(1)} %all-to-all-done.3.refs_12_.refs_4_) | copy-start | bytes 3932164
  67.0 21.8 %all-to-all-start.1 = ((bf16[8,256,256]{2,1,0:T(8,128)(2,1)}), bf16[8,256,256]{2,1,0:T(8,128)(2,1)S(1)}, u32[]{:S(2)}, u32[]{:S(2)}) async-start(bf16[8,256,256]{2,1,0:T(8,128)(2,1)} %shard_map.58), calls=%async_computation.1 | async-start | bytes 2097152 | tf_op jit(solution)/shard_map/all_to_all | solution.py:267
  88.8 68.6 %copy-start.2 = (bf16[8,256,256]{2,1,0:T(8,128)(2,1)}, bf16[8,256,256]{2,1,0:T(8,128)(2,1)S(1)}, u32[]{:S(2)}) copy-start(bf16[8,256,256]{2,1,0:T(8,128)(2,1)S(1)} %all-to-all-done.1.refs_0_) | copy-start | bytes 3145732
  88.8 68.6 %all-to-all-start.4 = ((bf16[16,608,256]{2,1,0:T(8,128)(2,1)}), bf16[16,608,256]{2,1,0:T(8,128)(2,1)}, u32[]{:S(2)}, u32[]{:S(2)}) async-start(bf16[16,608,256]{2,1,0:T(8,128)(2,1)} %slice.14), calls=%async_computation.4 | async-start | bytes 9961472 | tf_op jit(solution)/shard_map/all_to_all | solution.py:286
  95.5 66.9 %copy-start.9 = (s32[16,8]{0,1:T(8,128)S(1)}, s32[16,8]{0,1:T(8,128)}, u32[]{:S(2)}) copy-start(s32[16,8]{0,1:T(8,128)} %param.9) | copy-start | bytes 1540
  95.5 67.2 %copy-start.10 = (f32[1024]{0:T(1024)S(1)}, f32[1024]{0:T(1024)}, u32[]{:S(2)}) copy-start(f32[1024]{0:T(1024)} %param.8) | copy-start | bytes 12292
  95.6 25.8 %collective-permute-start.9 = (bf16[8,256,256]{2,1,0:T(8,128)(2,1)S(1)}, bf16[8,256,256]{2,1,0:T(8,128)(2,1)S(1)}, u32[]{:S(2)}, u32[]{:S(2)}) collective-permute-start(bf16[8,256,256]{2,1,0:T(8,128)(2,1)S(1)} %all-to-all-done.1.refs_0_), channel_id=1, source_target_pairs={{0,18},{2,16},{16,2},{18,0},{1,19},{3,17},{17,3},{19,1},{4,22},{6,... | collective-permute-start | bytes 3145736 | tf_op jit(solution)/shard_map/ppermute | solution.py:268
  98.3 25.4 %collective-permute-start.11 = (bf16[8,256,256]{2,1,0:T(8,128)(2,1)S(1)}, bf16[8,256,256]{2,1,0:T(8,128)(2,1)S(1)}, u32[]{:S(2)}, u32[]{:S(2)}) collective-permute-start(bf16[8,256,256]{2,1,0:T(8,128)(2,1)S(1)} %all-to-all-done.1.refs_0_), channel_id=1, source_target_pairs={{0,32},{32,64},{64,96},{96,0},{1,33},{33,65},{65,97},{97,1},{2,34}... | collective-permute-start | bytes 3145736 | tf_op jit(solution)/shard_map/ppermute | solution.py:17
  98.8 26.3 %collective-permute-start.13 = (bf16[8,256,256]{2,1,0:T(8,128)(2,1)S(1)}, bf16[8,256,256]{2,1,0:T(8,128)(2,1)S(1)}, u32[]{:S(2)}, u32[]{:S(2)}) collective-permute-start(bf16[8,256,256]{2,1,0:T(8,128)(2,1)S(1)} %all-to-all-done.1.refs_0_), channel_id=1, source_target_pairs={{0,96},{32,0},{64,32},{96,64},{1,97},{33,1},{65,33},{97,65},{2,98}... | collective-permute-start | bytes 3145736 | tf_op jit(solution)/shard_map/ppermute | solution.py:17
  100.9 24.2 %collective-permute-start.8 = (bf16[8,256,256]{2,1,0:T(8,128)(2,1)S(1)}, bf16[8,256,256]{2,1,0:T(8,128)(2,1)S(1)}, u32[]{:S(2)}, u32[]{:S(2)}) collective-permute-start(bf16[8,256,256]{2,1,0:T(8,128)(2,1)S(1)} %all-to-all-done.1.refs_0_), channel_id=1, source_target_pairs={{0,1},{1,0},{2,3},{3,2},{4,5},{5,4},{6,7},{7,6},{8,9},{9,8},{10,11... | collective-permute-start | bytes 3145736 | tf_op jit(solution)/shard_map/ppermute | solution.py:28
  121.4 3.8 %copy-start.3 = (bf16[8,256,256]{2,1,0:T(8,128)(2,1)}, bf16[8,256,256]{2,1,0:T(8,128)(2,1)S(1)}, u32[]{:S(2)}) copy-start(bf16[8,256,256]{2,1,0:T(8,128)(2,1)S(1)} %collective-permute-done.9.refs_2_) | copy-start | bytes 3145732
  121.4 23.8 %collective-permute-start.17 = (bf16[8,256,256]{2,1,0:T(8,128)(2,1)S(1)}, bf16[8,256,256]{2,1,0:T(8,128)(2,1)}, u32[]{:S(2)}, u32[]{:S(2)}) collective-permute-start(bf16[8,256,256]{2,1,0:T(8,128)(2,1)S(1)} %collective-permute-done.9.refs_2_), channel_id=1, source_target_pairs={{0,96},{32,0},{64,32},{96,64},{1,97},{33,1},{65,33},{97,65},{2,98}... | collective-permute-start | bytes 3145736 | tf_op jit(solution)/shard_map/ppermute | solution.py:17
  123.7 25.0 %collective-permute-start.15 = (bf16[8,256,256]{2,1,0:T(8,128)(2,1)S(1)}, bf16[8,256,256]{2,1,0:T(8,128)(2,1)}, u32[]{:S(2)}, u32[]{:S(2)}) collective-permute-start(bf16[8,256,256]{2,1,0:T(8,128)(2,1)S(1)} %collective-permute-done.9.refs_2_), channel_id=1, source_target_pairs={{0,32},{32,64},{64,96},{96,0},{1,33},{33,65},{65,97},{97,1},{2,34}... | collective-permute-start | bytes 3145736 | tf_op jit(solution)/shard_map/ppermute | solution.py:17
  123.7 33.8 %copy-start.4 = (bf16[8,256,256]{2,1,0:T(8,128)(2,1)}, bf16[8,256,256]{2,1,0:T(8,128)(2,1)S(1)}, u32[]{:S(2)}) copy-start(bf16[8,256,256]{2,1,0:T(8,128)(2,1)S(1)} %collective-permute-done.11.refs_4_) | copy-start | bytes 3145732
  123.7 28.6 %collective-permute-start.10 = (bf16[8,256,256]{2,1,0:T(8,128)(2,1)S(1)}, bf16[8,256,256]{2,1,0:T(8,128)(2,1)S(1)}, u32[]{:S(2)}, u32[]{:S(2)}) collective-permute-start(bf16[8,256,256]{2,1,0:T(8,128)(2,1)S(1)} %collective-permute-done.9.refs_2_), channel_id=1, source_target_pairs={{0,1},{1,0},{2,3},{3,2},{4,5},{5,4},{6,7},{7,6},{8,9},{9,8},{10,11... | collective-permute-start | bytes 3145736 | tf_op jit(solution)/shard_map/ppermute | solution.py:28
  125.1 45.8 %copy-start.5 = (bf16[8,256,256]{2,1,0:T(8,128)(2,1)}, bf16[8,256,256]{2,1,0:T(8,128)(2,1)S(1)}, u32[]{:S(2)}) copy-start(bf16[8,256,256]{2,1,0:T(8,128)(2,1)S(1)} %collective-permute-done.13.refs_6_) | copy-start | bytes 3145732
  125.1 27.3 %collective-permute-start.12 = (bf16[8,256,256]{2,1,0:T(8,128)(2,1)S(1)}, bf16[8,256,256]{2,1,0:T(8,128)(2,1)S(1)}, u32[]{:S(2)}, u32[]{:S(2)}) collective-permute-start(bf16[8,256,256]{2,1,0:T(8,128)(2,1)S(1)} %collective-permute-done.11.refs_4_), channel_id=1, source_target_pairs={{0,1},{1,0},{2,3},{3,2},{4,5},{5,4},{6,7},{7,6},{8,9},{9,8},{10,11... | collective-permute-start | bytes 3145736 | tf_op jit(solution)/shard_map/ppermute | solution.py:28
  125.2 27.2 %copy-start.6 = (bf16[8,256,256]{2,1,0:T(8,128)(2,1)}, bf16[8,256,256]{2,1,0:T(8,128)(2,1)S(1)}, u32[]{:S(2)}) copy-start(bf16[8,256,256]{2,1,0:T(8,128)(2,1)S(1)} %collective-permute-done.8.refs_1_) | copy-start | bytes 3145732
  125.2 45.7 %collective-permute-start.19 = (bf16[8,256,256]{2,1,0:T(8,128)(2,1)S(1)}, bf16[8,256,256]{2,1,0:T(8,128)(2,1)}, u32[]{:S(2)}, u32[]{:S(2)}) collective-permute-start(bf16[8,256,256]{2,1,0:T(8,128)(2,1)S(1)} %collective-permute-done.11.refs_4_), channel_id=1, source_target_pairs={{0,32},{32,64},{64,96},{96,0},{1,33},{33,65},{65,97},{97,1},{2,34}... | collective-permute-start | bytes 3145736 | tf_op jit(solution)/shard_map/ppermute | solution.py:17
  145.2 27.9 %collective-permute-start.21 = (bf16[8,256,256]{2,1,0:T(8,128)(2,1)}, bf16[8,256,256]{2,1,0:T(8,128)(2,1)}, u32[]{:S(2)}, u32[]{:S(2)}) collective-permute-start(bf16[8,256,256]{2,1,0:T(8,128)(2,1)} %collective-permute-done.17.refs_10_), channel_id=1, source_target_pairs={{0,96},{32,0},{64,32},{96,64},{1,97},{33,1},{65,33},{97,65},{2,98}... | collective-permute-start | bytes 3145736 | tf_op jit(solution)/shard_map/ppermute | solution.py:17
  148.7 25.3 %collective-permute-start.14 = (bf16[8,256,256]{2,1,0:T(8,128)(2,1)S(1)}, bf16[8,256,256]{2,1,0:T(8,128)(2,1)}, u32[]{:S(2)}, u32[]{:S(2)}) collective-permute-start(bf16[8,256,256]{2,1,0:T(8,128)(2,1)S(1)} %collective-permute-done.13.refs_6_), channel_id=1, source_target_pairs={{0,1},{1,0},{2,3},{3,2},{4,5},{5,4},{6,7},{7,6},{8,9},{9,8},{10,11... | collective-permute-start | bytes 3145736 | tf_op jit(solution)/shard_map/ppermute | solution.py:28
  152.3 1.0 copy-start.7
  152.3 21.6 %collective-permute-start.18 = (bf16[8,256,256]{2,1,0:T(8,128)(2,1)}, bf16[8,256,256]{2,1,0:T(8,128)(2,1)}, u32[]{:S(2)}, u32[]{:S(2)}) collective-permute-start(bf16[8,256,256]{2,1,0:T(8,128)(2,1)} %collective-permute-done.17.refs_10_), channel_id=1, source_target_pairs={{0,1},{1,0},{2,3},{3,2},{4,5},{5,4},{6,7},{7,6},{8,9},{9,8},{10,11... | collective-permute-start | bytes 3145736 | tf_op jit(solution)/shard_map/ppermute | solution.py:28
  153.3 1.0 copy-start.8
  154.3 19.7 %collective-permute-start.16 = (bf16[8,256,256]{2,1,0:T(8,128)(2,1)}, bf16[8,256,256]{2,1,0:T(8,128)(2,1)}, u32[]{:S(2)}, u32[]{:S(2)}) collective-permute-start(bf16[8,256,256]{2,1,0:T(8,128)(2,1)} %collective-permute-done.15.refs_8_), channel_id=1, source_target_pairs={{0,1},{1,0},{2,3},{3,2},{4,5},{5,4},{6,7},{7,6},{8,9},{9,8},{10,11... | collective-permute-start | bytes 3145736 | tf_op jit(solution)/shard_map/ppermute | solution.py:28
  157.5 42.8 %all-to-all-start.2 = ((bf16[16,256,256]{2,1,0:T(8,128)(2,1)}), bf16[16,256,256]{2,1,0:T(8,128)(2,1)}, u32[]{:S(2)}, u32[]{:S(2)}) async-start(bf16[16,256,256]{2,1,0:T(8,128)(2,1)} %slice.12), calls=%async_computation.2 | async-start | bytes 4194304 | tf_op jit(solution)/shard_map/all_to_all | solution.py:286
  170.9 20.0 %collective-permute-start.20 = (bf16[8,256,256]{2,1,0:T(8,128)(2,1)}, bf16[8,256,256]{2,1,0:T(8,128)(2,1)}, u32[]{:S(2)}, u32[]{:S(2)}) collective-permute-start(bf16[8,256,256]{2,1,0:T(8,128)(2,1)} %collective-permute-done.19.refs_0_.refs_12_), channel_id=1, source_target_pairs={{0,1},{1,0},{2,3},{3,2},{4,5},{5,4},{6,7},{7,6},{8,9},{9,8},{10,11... | collective-permute-start | bytes 3145736 | tf_op jit(solution)/shard_map/ppermute | solution.py:28
  173.0 17.9 %collective-permute-start.22 = (bf16[8,256,256]{2,1,0:T(8,128)(2,1)}, bf16[8,256,256]{2,1,0:T(8,128)(2,1)}, u32[]{:S(2)}, u32[]{:S(2)}) collective-permute-start(bf16[8,256,256]{2,1,0:T(8,128)(2,1)} %collective-permute-done.21.refs_2_.refs_14_), channel_id=1, source_target_pairs={{0,1},{1,0},{2,3},{3,2},{4,5},{5,4},{6,7},{7,6},{8,9},{9,8},{10,11... | collective-permute-start | bytes 3145736 | tf_op jit(solution)/shard_map/ppermute | solution.py:28

commit v4 on v3

--- a/solution.py
+++ b/solution.py
@@ -7,7 +7,7 @@
 
 BLK = 128
 PB = ("z", "xl", "c")
-WIDTHS = (160, 608, 256)
+WIDTHS = (160, 480, 384)
 
 IN_VMEM = pl.BlockSpec(memory_space=pltpu.VMEM)
 ANYWHERE = pl.BlockSpec(memory_space=pl.ANY)
@@ -137,12 +137,13 @@
         load(0, 0, half).start()
     for k in range(jobs[0][2], jobs[0][3]):
         fetches[k].start()
+    if m > 1:
+        for k in pending:
+            fetches[k].wait()
+        pending = []
     for k in range(1, min(slots - 1, n)):
         for half in range(2):
             load(k, k, half).start()
-    for k in range(m):
-        if not jobs[0][2] <= k < jobs[0][3]:
-            fetches[k].start()
 
     for number, (low, high, start, stop) in enumerate(jobs):
         left, width, ready = at[start], at[stop] - at[start], readies[number]
@@ -230,9 +231,9 @@
         out_specs=ANYWHERE,
         out_shape=jax.ShapeDtypeStruct(total, jnp.float32),
         scratch_shapes=[
-            pltpu.VMEM((3, 2, pieces, rows, cols), jnp.bfloat16),
+            pltpu.VMEM((5, 2, pieces, rows, cols), jnp.bfloat16),
             pltpu.VMEM((16, sum(widths), cols), jnp.bfloat16),
-            pltpu.SemaphoreType.DMA((3, 2)),
+            pltpu.SemaphoreType.DMA((5, 2)),
             pltpu.SemaphoreType.DMA((len(trains),)),
             pltpu.SemaphoreType.DMA((len(jobs), 2)),
         ]

time: 212 us -> 216 us (1.019)
  waiting for transfers between devices: 89.2 us -> 96.8 us
  starting transfers between devices: 66.5 us -> 61.2 us
  Pallas kernels: 41 us -> 43.3 us
    all_to_all x3, waiting for transfers between devices: 0.01 us -> 12.4 us  [on_device(): lax.all_to_all(cut, PB, split_axis=0, concat_axis=0, tiled=True)]
    ppermute x6, waiting for transfers between devices: 27.2 us -> 21.8 us  [shift(): return lax.ppermute(x, 'y', [(i, (i + by) % 4) for i in range(4)])]
    ppermute x9, starting transfers between devices: 10.9 us -> 7.27 us  [swap(): return lax.ppermute(x, 'c', [(0, 1), (1, 0)])]
    pallas_call x3, Pallas kernels: 37.1 us -> 39.4 us  [scores(): pl.pallas_call(lambda *refs: score_kernel(places, widths, jobs, first, *r...]
  transfers between devices with their start and end apart: 28 -> 28, of which waited for: 8 -> 8; matrix products, arithmetic and copies ran while one was open for 5% -> 5% of each run, Pallas kernels for 13% -> 12%
where the time goes in v4:
time: 216 us; the launch traced here: 215 us
  waiting for transfers between devices  96.8 us (45%)
  starting transfers between devices  61.2 us (28%)
  Pallas kernels  43.3 us (20%)
  local copies, waits for them, and re-layouts  12.7 us (6%)
    pallas_call x3, Pallas kernels, scores(): pl.pallas_call(lambda *refs: score_kernel(places, widths, jobs, first, *r...  39.4 us
    ppermute x6, waiting for transfers between devices, ring(): got[by] = lax.ppermute(x, axis, [(i, (i + by) % 4) for i in range(4)])  24.2 us
    ppermute x6, waiting for transfers between devices, shift(): return lax.ppermute(x, 'y', [(i, (i + by) % 4) for i in range(4)])  21.8 us
    ppermute x1, waiting for transfers between devices, on_device(): other = lax.ppermute(plane, ('xh', 'xl'), [(0, 3), (1, 2), (2, 1), (3, 0)])  19.1 us
    all_to_all x3, starting transfers between devices, on_device(): lax.all_to_all(cut, PB, split_axis=0, concat_axis=0, tiled=True)  17.1 us
    all_to_all x3, waiting for transfers between devices, on_device(): lax.all_to_all(cut, PB, split_axis=0, concat_axis=0, tiled=True)  12.4 us
    slice x3, local copies, waits for them, and re-layouts, on_device(): cuts.append(pieces[:, start:start + width])  10.7 us
    all_to_all x1, waiting for transfers between devices, on_device(): lax.all_to_all(tile, ('z', 'xl'), split_axis=0, concat_axis=0, tiled=True)  9.99 us
  transfers between devices with their start and end apart: 28, of which 8 were waited for; matrix products, arithmetic and copies ran while one was open for 5% of the time, Pallas kernels for 12%

profile of v4, /device:TPU:1, one launch (start us, length us, event | category | flops | bytes accessed | tf_op | source)
XLA Modules:
  0.0 215.0 jit_solution(4349309065535230665)
XLA Ops:
  0.0 2.0 shard_map.55
  2.0 7.8 %all-to-all-start = ((bf16[16,64,256]{2,1,0:T(8,128)(2,1)}), bf16[16,64,256]{2,1,0:T(8,128)(2,1)S(1)}, u32[]{:S(2)}, u32[]{:S(2)}) async-start(bf16[16,64,256]{2,1,0:T(8,128)(2,1)} %shard_map.55), calls=%async_computation | async-start | bytes 1048576 | tf_op jit(solution)/shard_map/all_to_all | solution.py:259
  9.7 1.4 collective-permute-start.3
  11.1 9.3 %collective-permute-done.3.refs_1_ = bf16[256,256]{1,0:T(8,128)(2,1)S(1)} collective-permute-done((bf16[256,256]{1,0:T(8,128)(2,1)}, bf16[256,256]{1,0:T(8,128)(2,1)S(1)}, u32[]{:S(2)}, u32[]{:S(2)}) %collective-permute-start.3) | collective-permute-done | bytes 131104 | tf_op jit(solution)/shard_map/ppermute | solution.py:261
  20.4 0.9 copy-done
  21.3 1.3 collective-permute-start.4
  22.5 2.4 %collective-permute-start.5 = (bf16[2,256,256]{2,1,0:T(8,128)(2,1)S(1)}, bf16[2,256,256]{2,1,0:T(8,128)(2,1)S(1)}, u32[]{:S(2)}, u32[]{:S(2)}) collective-permute-start(bf16[2,256,256]{2,1,0:T(8,128)(2,1)S(1)} %shard_map.56.refs_0_), channel_id=1, source_target_pairs={{0,8},{4,12},{8,0},{12,4},{1,9},{5,13},{9,1},{13,5},{2,10},{6,14},... | collective-permute-start | bytes 786440 | tf_op jit(solution)/shard_map/ppermute | solution.py:23
  24.9 1.2 collective-permute-start.6
  26.1 2.5 %slice.13 = bf16[16,160,256]{2,1,0:T(8,128)(2,1)} slice(bf16[16,1024,256]{2,1,0:T(8,128)(2,1)} %bitcast.1), slice={[0:16], [0:160], [0:256]} | slice | bytes 2621440 | tf_op jit(solution)/shard_map/slice | solution.py:257
  28.6 5.3 %all-to-all-start.3 = ((bf16[16,160,256]{2,1,0:T(8,128)(2,1)}), bf16[16,160,256]{2,1,0:T(8,128)(2,1)S(1)}, u32[]{:S(2)}, u32[]{:S(2)}) async-start(bf16[16,160,256]{2,1,0:T(8,128)(2,1)} %slice.13), calls=%async_computation.3 | async-start | bytes 2621440 | tf_op jit(solution)/shard_map/all_to_all | solution.py:287
  33.9 2.1 collective-permute-done.5.refs_2_
  36.0 0.1 shard_map.57.refs_4_
  36.1 2.0 collective-permute-start.7
  38.1 1.3 collective-permute-start
  39.4 2.6 %collective-permute-start.1 = (bf16[16,64,256]{2,1,0:T(8,128)(2,1)S(1)}, bf16[16,64,256]{2,1,0:T(8,128)(2,1)S(1)}, u32[]{:S(2)}, u32[]{:S(2)}) collective-permute-start(bf16[16,64,256]{2,1,0:T(8,128)(2,1)S(1)} %all-to-all-done.refs_0_), channel_id=1, source_target_pairs={{0,64},{32,96},{64,0},{96,32},{1,65},{33,97},{65,1},{97,33},{2,66}... | collective-permute-start | bytes 1572872 | tf_op jit(solution)/shard_map/ppermute | solution.py:23
  42.0 1.1 collective-permute-start.2
  43.1 9.7 %collective-permute-done.refs_1_ = bf16[16,64,256]{2,1,0:T(8,128)(2,1)S(1)} collective-permute-done((bf16[16,64,256]{2,1,0:T(8,128)(2,1)S(1)}, bf16[16,64,256]{2,1,0:T(8,128)(2,1)S(1)}, u32[]{:S(2)}, u32[]{:S(2)}) %collective-permute-start) | collective-permute-done | bytes 524320 | tf_op jit(solution)/shard_map/ppermute | solution.py:23
  52.8 12.4 %collective-permute-done.1.refs_2_ = bf16[16,64,256]{2,1,0:T(8,128)(2,1)S(1)} collective-permute-done((bf16[16,64,256]{2,1,0:T(8,128)(2,1)S(1)}, bf16[16,64,256]{2,1,0:T(8,128)(2,1)S(1)}, u32[]{:S(2)}, u32[]{:S(2)}) %collective-permute-start.1) | collective-permute-done | bytes 524320 | tf_op jit(solution)/shard_map/ppermute | solution.py:23
  65.2 1.8 shard_map.58
  67.0 7.5 %all-to-all-start.1 = ((bf16[8,256,256]{2,1,0:T(8,128)(2,1)}), bf16[8,256,256]{2,1,0:T(8,128)(2,1)S(1)}, u32[]{:S(2)}, u32[]{:S(2)}) async-start(bf16[8,256,256]{2,1,0:T(8,128)(2,1)} %shard_map.58), calls=%async_computation.1 | async-start | bytes 2097152 | tf_op jit(solution)/shard_map/all_to_all | solution.py:268
  74.6 4.3 %slice.14 = bf16[16,480,256]{2,1,0:T(8,128)(2,1)} slice(bf16[16,1024,256]{2,1,0:T(8,128)(2,1)} %bitcast.2), slice={[0:16], [160:640], [0:256]} | slice | bytes 7864320 | tf_op jit(solution)/shard_map/slice | solution.py:257
  78.8 10.0 %all-to-all-done.1.refs_0_ = bf16[8,256,256]{2,1,0:T(8,128)(2,1)S(1)} async-done(((bf16[8,256,256]{2,1,0:T(8,128)(2,1)}), bf16[8,256,256]{2,1,0:T(8,128)(2,1)S(1)}, u32[]{:S(2)}, u32[]{:S(2)}) %all-to-all-start.1) | async-done | bytes 1048608 | tf_op jit(solution)/shard_map/all_to_all | solution.py:268
  88.8 6.6 %all-to-all-start.4 = ((bf16[16,480,256]{2,1,0:T(8,128)(2,1)}), bf16[16,480,256]{2,1,0:T(8,128)(2,1)}, u32[]{:S(2)}, u32[]{:S(2)}) async-start(bf16[16,480,256]{2,1,0:T(8,128)(2,1)} %slice.14), calls=%async_computation.4 | async-start | bytes 7864320 | tf_op jit(solution)/shard_map/all_to_all | solution.py:287
  95.5 2.6 %collective-permute-start.9 = (bf16[8,256,256]{2,1,0:T(8,128)(2,1)S(1)}, bf16[8,256,256]{2,1,0:T(8,128)(2,1)S(1)}, u32[]{:S(2)}, u32[]{:S(2)}) collective-permute-start(bf16[8,256,256]{2,1,0:T(8,128)(2,1)S(1)} %all-to-all-done.1.refs_0_), channel_id=1, source_target_pairs={{0,18},{2,16},{16,2},{18,0},{1,19},{3,17},{17,3},{19,1},{4,22},{6,... | collective-permute-start | bytes 3145736 | tf_op jit(solution)/shard_map/ppermute | solution.py:269
  98.1 0.5 collective-permute-start.11
  98.6 2.2 %collective-permute-start.13 = (bf16[8,256,256]{2,1,0:T(8,128)(2,1)S(1)}, bf16[8,256,256]{2,1,0:T(8,128)(2,1)S(1)}, u32[]{:S(2)}, u32[]{:S(2)}) collective-permute-start(bf16[8,256,256]{2,1,0:T(8,128)(2,1)S(1)} %all-to-all-done.1.refs_0_), channel_id=1, source_target_pairs={{0,96},{32,0},{64,32},{96,64},{1,97},{33,1},{65,33},{97,65},{2,98}... | collective-permute-start | bytes 3145736 | tf_op jit(solution)/shard_map/ppermute | solution.py:17
  100.8 1.2 collective-permute-start.8
  102.0 19.1 %collective-permute-done.9.refs_2_ = bf16[8,256,256]{2,1,0:T(8,128)(2,1)S(1)} collective-permute-done((bf16[8,256,256]{2,1,0:T(8,128)(2,1)S(1)}, bf16[8,256,256]{2,1,0:T(8,128)(2,1)S(1)}, u32[]{:S(2)}, u32[]{:S(2)}) %collective-permute-start.9) | collective-permute-done | bytes 1048608 | tf_op jit(solution)/shard_map/ppermute | solution.py:269
  121.2 2.3 %collective-permute-start.17 = (bf16[8,256,256]{2,1,0:T(8,128)(2,1)S(1)}, bf16[8,256,256]{2,1,0:T(8,128)(2,1)}, u32[]{:S(2)}, u32[]{:S(2)}) collective-permute-start(bf16[8,256,256]{2,1,0:T(8,128)(2,1)S(1)} %collective-permute-done.9.refs_2_), channel_id=1, source_target_pairs={{0,96},{32,0},{64,32},{96,64},{1,97},{33,1},{65,33},{97,65},{2,98}... | collective-permute-start | bytes 3145736 | tf_op jit(solution)/shard_map/ppermute | solution.py:17
  123.5 1.4 collective-permute-start.10
  124.9 1.0 copy-done.5
  125.9 0.1 collective-permute-start.12
  126.0 3.9 %slice.12 = bf16[16,384,256]{2,1,0:T(8,128)(2,1)} slice(bf16[16,1024,256]{2,1,0:T(8,128)(2,1)} %bitcast.3), slice={[0:16], [640:1024], [0:256]} | slice | bytes 6291456 | tf_op jit(solution)/shard_map/slice | solution.py:257
  129.9 12.4 %all-to-all-done.4.refs_13_.refs_5_ = bf16[16,480,256]{2,1,0:T(8,128)(2,1)} async-done(((bf16[16,480,256]{2,1,0:T(8,128)(2,1)}), bf16[16,480,256]{2,1,0:T(8,128)(2,1)}, u32[]{:S(2)}, u32[]{:S(2)}) %all-to-all-start.4) | async-done | bytes 3932192 | tf_op jit(solution)/shard_map/all_to_all | solution.py:287
  142.3 5.2 %all-to-all-start.2 = ((bf16[16,384,256]{2,1,0:T(8,128)(2,1)}), bf16[16,384,256]{2,1,0:T(8,128)(2,1)}, u32[]{:S(2)}, u32[]{:S(2)}) async-start(bf16[16,384,256]{2,1,0:T(8,128)(2,1)} %slice.12), calls=%async_computation.2 | async-start | bytes 6291456 | tf_op jit(solution)/shard_map/all_to_all | solution.py:287
  147.5 0.6 collective-permute-start.19
  148.1 2.2 %collective-permute-start.21 = (bf16[8,256,256]{2,1,0:T(8,128)(2,1)}, bf16[8,256,256]{2,1,0:T(8,128)(2,1)}, u32[]{:S(2)}, u32[]{:S(2)}) collective-permute-start(bf16[8,256,256]{2,1,0:T(8,128)(2,1)} %collective-permute-done.17.refs_10_), channel_id=1, source_target_pairs={{0,96},{32,0},{64,32},{96,64},{1,97},{33,1},{65,33},{97,65},{2,98}... | collective-permute-start | bytes 3145736 | tf_op jit(solution)/shard_map/ppermute | solution.py:17
  150.3 0.8 collective-permute-start.14
  151.1 0.1 collective-permute-start.18
  151.2 0.4 collective-permute-start.16
  151.6 21.7 %collective-permute-done.19.refs_0_.refs_12_ = bf16[8,256,256]{2,1,0:T(8,128)(2,1)} collective-permute-done((bf16[8,256,256]{2,1,0:T(8,128)(2,1)S(1)}, bf16[8,256,256]{2,1,0:T(8,128)(2,1)}, u32[]{:S(2)}, u32[]{:S(2)}) %collective-permute-start.19) | collective-permute-done | bytes 1048608 | tf_op jit(solution)/shard_map/ppermute | solution.py:17
  173.3 1.1 collective-permute-start.20
  174.5 0.1 copy.8
  174.6 0.1 broadcast_in_dim.4
  174.7 0.6 broadcast_multiply_fusion.refs_14_.refs_6_.refs_17_
  175.4 16.0 %shard_map.59.refs_7_ = f32[2048,1024]{1,0:T(8,128)} custom-call(bf16[8,256,256]{2,1,0:T(8,128)(2,1)} %copy-done.2, bf16[8,256,256]{2,1,0:T(8,128)(2,1)} %collective-permute-done.8.refs_1_, bf16[8,256,256]{2,1,0:T(8,128)(2,1)} %copy-done.3, bf16[8,256,256]{2,1,0:T(8,128)(2,1)} %collective-permute-done.10.refs_3_, bf16[8,256,256]{2,1,0:T(8,128)(2,1)} %copy-done.4, ...), custom_call_target="tpu_custom_call" | custom-call | flops 8053063680 | bytes 21757952 | tf_op jit(solution)/shard_map/pallas_call | solution.py:228
  191.4 8.6 %shard_map.60.refs_18_ = f32[2048,1024]{1,0:T(8,128)} custom-call(bf16[8,256,256]{2,1,0:T(8,128)(2,1)} %collective-permute-done.19.refs_0_.refs_12_, bf16[8,256,256]{2,1,0:T(8,128)(2,1)} %collective-permute-done.20.refs_1_.refs_13_, bf16[8,256,256]{2,1,0:T(8,128)(2,1)} %collective-permute-done.21.refs_2_.refs_14_, ...), custom_call_target="tpu_custom_call", output_to_operand_aliasing={{}: (7, {})} | custom-call | flops 2684354560 | bytes 10747904 | tf_op jit(solution)/shard_map/pallas_call | solution.py:228
  200.1 14.7 %shard_map.61 = f32[2048,1024]{1,0:T(8,128)} custom-call(bf16[8,256,256]{2,1,0:T(8,128)(2,1)} %copy-done.2, bf16[8,256,256]{2,1,0:T(8,128)(2,1)} %collective-permute-done.8.refs_1_, bf16[8,256,256]{2,1,0:T(8,128)(2,1)} %copy-done.3, bf16[8,256,256]{2,1,0:T(8,128)(2,1)} %collective-permute-done.10.refs_3_, ...), custom_call_target="tpu_custom_call", output_to_operand_aliasing={{}: (18, {})} | custom-call | flops 6442450944 | bytes 23068672 | tf_op jit(solution)/shard_map/pallas_call | solution.py:228
  (40 shorter events, 0.2 us)
Async XLA Ops:
  2.0 26.6 %all-to-all-start = ((bf16[16,64,256]{2,1,0:T(8,128)(2,1)}), bf16[16,64,256]{2,1,0:T(8,128)(2,1)S(1)}, u32[]{:S(2)}, u32[]{:S(2)}) async-start(bf16[16,64,256]{2,1,0:T(8,128)(2,1)} %shard_map.55), calls=%async_computation | async-start | bytes 1048576 | tf_op jit(solution)/shard_map/all_to_all | solution.py:259
  9.7 10.6 %collective-permute-start.3 = (bf16[256,256]{1,0:T(8,128)(2,1)}, bf16[256,256]{1,0:T(8,128)(2,1)S(1)}, u32[]{:S(2)}, u32[]{:S(2)}) collective-permute-start(bf16[256,256]{1,0:T(8,128)(2,1)} %refs_0_.1), channel_id=1, source_target_pairs={{0,2},{2,0},{1,3},{3,1},{4,6},{6,4},{5,7},{7,5},{8,10},{10,8},{9,1... | collective-permute-start | bytes 393224 | tf_op jit(solution)/shard_map/ppermute | solution.py:261
  20.4 0.9 copy-start
  21.3 12.6 %collective-permute-start.4 = (bf16[2,256,256]{2,1,0:T(8,128)(2,1)S(1)}, bf16[2,256,256]{2,1,0:T(8,128)(2,1)S(1)}, u32[]{:S(2)}, u32[]{:S(2)}) collective-permute-start(bf16[2,256,256]{2,1,0:T(8,128)(2,1)S(1)} %shard_map.56.refs_0_), channel_id=1, source_target_pairs={{0,4},{4,8},{8,12},{12,0},{1,5},{5,9},{9,13},{13,1},{2,6},{6,10},{... | collective-permute-start | bytes 786440 | tf_op jit(solution)/shard_map/ppermute | solution.py:23
  22.5 13.4 %collective-permute-start.5 = (bf16[2,256,256]{2,1,0:T(8,128)(2,1)S(1)}, bf16[2,256,256]{2,1,0:T(8,128)(2,1)S(1)}, u32[]{:S(2)}, u32[]{:S(2)}) collective-permute-start(bf16[2,256,256]{2,1,0:T(8,128)(2,1)S(1)} %shard_map.56.refs_0_), channel_id=1, source_target_pairs={{0,8},{4,12},{8,0},{12,4},{1,9},{5,13},{9,1},{13,5},{2,10},{6,14},... | collective-permute-start | bytes 786440 | tf_op jit(solution)/shard_map/ppermute | solution.py:23
  24.9 11.0 %collective-permute-start.6 = (bf16[2,256,256]{2,1,0:T(8,128)(2,1)S(1)}, bf16[2,256,256]{2,1,0:T(8,128)(2,1)S(1)}, u32[]{:S(2)}, u32[]{:S(2)}) collective-permute-start(bf16[2,256,256]{2,1,0:T(8,128)(2,1)S(1)} %shard_map.56.refs_0_), channel_id=1, source_target_pairs={{0,12},{4,0},{8,4},{12,8},{1,13},{5,1},{9,5},{13,9},{2,14},{6,2},{... | collective-permute-start | bytes 786440 | tf_op jit(solution)/shard_map/ppermute | solution.py:23
  28.6 38.4 %all-to-all-start.3 = ((bf16[16,160,256]{2,1,0:T(8,128)(2,1)}), bf16[16,160,256]{2,1,0:T(8,128)(2,1)S(1)}, u32[]{:S(2)}, u32[]{:S(2)}) async-start(bf16[16,160,256]{2,1,0:T(8,128)(2,1)} %slice.13), calls=%async_computation.3 | async-start | bytes 2621440 | tf_op jit(solution)/shard_map/all_to_all | solution.py:287
  36.1 29.1 %collective-permute-start.7 = (bf16[8,256,256]{2,1,0:T(8,128)(2,1)S(1)}, bf16[8,256,256]{2,1,0:T(8,128)(2,1)S(1)}, u32[]{:S(2)}, u32[]{:S(2)}) collective-permute-start(bf16[8,256,256]{2,1,0:T(8,128)(2,1)S(1)} %shard_map.57.refs_4_), channel_id=1, source_target_pairs={{0,1},{1,0},{2,3},{3,2},{4,5},{5,4},{6,7},{7,6},{8,9},{9,8},{10,11... | collective-permute-start | bytes 3145736 | tf_op jit(solution)/shard_map/ppermute | solution.py:28
  38.1 14.7 %collective-permute-start = (bf16[16,64,256]{2,1,0:T(8,128)(2,1)S(1)}, bf16[16,64,256]{2,1,0:T(8,128)(2,1)S(1)}, u32[]{:S(2)}, u32[]{:S(2)}) collective-permute-start(bf16[16,64,256]{2,1,0:T(8,128)(2,1)S(1)} %all-to-all-done.refs_0_), channel_id=1, source_target_pairs={{0,32},{32,64},{64,96},{96,0},{1,33},{33,65},{65,97},{97,1},{2,34}... | collective-permute-start | bytes 1572872 | tf_op jit(solution)/shard_map/ppermute | solution.py:23
  39.4 25.8 %collective-permute-start.1 = (bf16[16,64,256]{2,1,0:T(8,128)(2,1)S(1)}, bf16[16,64,256]{2,1,0:T(8,128)(2,1)S(1)}, u32[]{:S(2)}, u32[]{:S(2)}) collective-permute-start(bf16[16,64,256]{2,1,0:T(8,128)(2,1)S(1)} %all-to-all-done.refs_0_), channel_id=1, source_target_pairs={{0,64},{32,96},{64,0},{96,32},{1,65},{33,97},{65,1},{97,33},{2,66}... | collective-permute-start | bytes 1572872 | tf_op jit(solution)/shard_map/ppermute | solution.py:23
  42.0 23.2 %collective-permute-start.2 = (bf16[16,64,256]{2,1,0:T(8,128)(2,1)S(1)}, bf16[16,64,256]{2,1,0:T(8,128)(2,1)S(1)}, u32[]{:S(2)}, u32[]{:S(2)}) collective-permute-start(bf16[16,64,256]{2,1,0:T(8,128)(2,1)S(1)} %all-to-all-done.refs_0_), channel_id=1, source_target_pairs={{0,96},{32,0},{64,32},{96,64},{1,97},{33,1},{65,33},{97,65},{2,98}... | collective-permute-start | bytes 1572872 | tf_op jit(solution)/shard_map/ppermute | solution.py:23
  67.0 11.8 %copy-start.1 = (bf16[16,160,256]{2,1,0:T(8,128)(2,1)}, bf16[16,160,256]{2,1,0:T(8,128)(2,1)S(1)}, u32[]{:S(2)}) copy-start(bf16[16,160,256]{2,1,0:T(8,128)(2,1)S(1)} %all-to-all-done.3.refs_12_.refs_4_) | copy-start | bytes 3932164
  67.0 21.8 %all-to-all-start.1 = ((bf16[8,256,256]{2,1,0:T(8,128)(2,1)}), bf16[8,256,256]{2,1,0:T(8,128)(2,1)S(1)}, u32[]{:S(2)}, u32[]{:S(2)}) async-start(bf16[8,256,256]{2,1,0:T(8,128)(2,1)} %shard_map.58), calls=%async_computation.1 | async-start | bytes 2097152 | tf_op jit(solution)/shard_map/all_to_all | solution.py:268
  88.8 41.0 %copy-start.2 = (bf16[8,256,256]{2,1,0:T(8,128)(2,1)}, bf16[8,256,256]{2,1,0:T(8,128)(2,1)S(1)}, u32[]{:S(2)}) copy-start(bf16[8,256,256]{2,1,0:T(8,128)(2,1)S(1)} %all-to-all-done.1.refs_0_) | copy-start | bytes 3145732
  88.8 53.4 %all-to-all-start.4 = ((bf16[16,480,256]{2,1,0:T(8,128)(2,1)}), bf16[16,480,256]{2,1,0:T(8,128)(2,1)}, u32[]{:S(2)}, u32[]{:S(2)}) async-start(bf16[16,480,256]{2,1,0:T(8,128)(2,1)} %slice.14), calls=%async_computation.4 | async-start | bytes 7864320 | tf_op jit(solution)/shard_map/all_to_all | solution.py:287
  95.5 25.7 %collective-permute-start.9 = (bf16[8,256,256]{2,1,0:T(8,128)(2,1)S(1)}, bf16[8,256,256]{2,1,0:T(8,128)(2,1)S(1)}, u32[]{:S(2)}, u32[]{:S(2)}) collective-permute-start(bf16[8,256,256]{2,1,0:T(8,128)(2,1)S(1)} %all-to-all-done.1.refs_0_), channel_id=1, source_target_pairs={{0,18},{2,16},{16,2},{18,0},{1,19},{3,17},{17,3},{19,1},{4,22},{6,... | collective-permute-start | bytes 3145736 | tf_op jit(solution)/shard_map/ppermute | solution.py:269
  98.1 25.4 %collective-permute-start.11 = (bf16[8,256,256]{2,1,0:T(8,128)(2,1)S(1)}, bf16[8,256,256]{2,1,0:T(8,128)(2,1)S(1)}, u32[]{:S(2)}, u32[]{:S(2)}) collective-permute-start(bf16[8,256,256]{2,1,0:T(8,128)(2,1)S(1)} %all-to-all-done.1.refs_0_), channel_id=1, source_target_pairs={{0,32},{32,64},{64,96},{96,0},{1,33},{33,65},{65,97},{97,1},{2,34}... | collective-permute-start | bytes 3145736 | tf_op jit(solution)/shard_map/ppermute | solution.py:17
  98.6 26.3 %collective-permute-start.13 = (bf16[8,256,256]{2,1,0:T(8,128)(2,1)S(1)}, bf16[8,256,256]{2,1,0:T(8,128)(2,1)S(1)}, u32[]{:S(2)}, u32[]{:S(2)}) collective-permute-start(bf16[8,256,256]{2,1,0:T(8,128)(2,1)S(1)} %all-to-all-done.1.refs_0_), channel_id=1, source_target_pairs={{0,96},{32,0},{64,32},{96,64},{1,97},{33,1},{65,33},{97,65},{2,98}... | collective-permute-start | bytes 3145736 | tf_op jit(solution)/shard_map/ppermute | solution.py:17
  100.8 46.7 %collective-permute-start.8 = (bf16[8,256,256]{2,1,0:T(8,128)(2,1)S(1)}, bf16[8,256,256]{2,1,0:T(8,128)(2,1)}, u32[]{:S(2)}, u32[]{:S(2)}) collective-permute-start(bf16[8,256,256]{2,1,0:T(8,128)(2,1)S(1)} %all-to-all-done.1.refs_0_), channel_id=1, source_target_pairs={{0,1},{1,0},{2,3},{3,2},{4,5},{5,4},{6,7},{7,6},{8,9},{9,8},{10,11... | collective-permute-start | bytes 3145736 | tf_op jit(solution)/shard_map/ppermute | solution.py:28
  121.1 21.1 %copy-start.3 = (bf16[8,256,256]{2,1,0:T(8,128)(2,1)}, bf16[8,256,256]{2,1,0:T(8,128)(2,1)S(1)}, u32[]{:S(2)}) copy-start(bf16[8,256,256]{2,1,0:T(8,128)(2,1)S(1)} %collective-permute-done.9.refs_2_) | copy-start | bytes 3145732
  121.2 26.9 %collective-permute-start.17 = (bf16[8,256,256]{2,1,0:T(8,128)(2,1)S(1)}, bf16[8,256,256]{2,1,0:T(8,128)(2,1)}, u32[]{:S(2)}, u32[]{:S(2)}) collective-permute-start(bf16[8,256,256]{2,1,0:T(8,128)(2,1)S(1)} %collective-permute-done.9.refs_2_), channel_id=1, source_target_pairs={{0,96},{32,0},{64,32},{96,64},{1,97},{33,1},{65,33},{97,65},{2,98}... | collective-permute-start | bytes 3145736 | tf_op jit(solution)/shard_map/ppermute | solution.py:17
  123.4 26.8 %collective-permute-start.15 = (bf16[8,256,256]{2,1,0:T(8,128)(2,1)S(1)}, bf16[8,256,256]{2,1,0:T(8,128)(2,1)}, u32[]{:S(2)}, u32[]{:S(2)}) collective-permute-start(bf16[8,256,256]{2,1,0:T(8,128)(2,1)S(1)} %collective-permute-done.9.refs_2_), channel_id=1, source_target_pairs={{0,32},{32,64},{64,96},{96,0},{1,33},{33,65},{65,97},{97,1},{2,34}... | collective-permute-start | bytes 3145736 | tf_op jit(solution)/shard_map/ppermute | solution.py:17
  123.5 24.0 %copy-start.4 = (bf16[8,256,256]{2,1,0:T(8,128)(2,1)}, bf16[8,256,256]{2,1,0:T(8,128)(2,1)S(1)}, u32[]{:S(2)}) copy-start(bf16[8,256,256]{2,1,0:T(8,128)(2,1)S(1)} %collective-permute-done.11.refs_4_) | copy-start | bytes 3145732
  123.5 27.6 %collective-permute-start.10 = (bf16[8,256,256]{2,1,0:T(8,128)(2,1)S(1)}, bf16[8,256,256]{2,1,0:T(8,128)(2,1)}, u32[]{:S(2)}, u32[]{:S(2)}) collective-permute-start(bf16[8,256,256]{2,1,0:T(8,128)(2,1)S(1)} %collective-permute-done.9.refs_2_), channel_id=1, source_target_pairs={{0,1},{1,0},{2,3},{3,2},{4,5},{5,4},{6,7},{7,6},{8,9},{9,8},{10,11... | collective-permute-start | bytes 3145736 | tf_op jit(solution)/shard_map/ppermute | solution.py:28
  124.9 1.0 copy-start.5
  125.9 25.3 %collective-permute-start.12 = (bf16[8,256,256]{2,1,0:T(8,128)(2,1)S(1)}, bf16[8,256,256]{2,1,0:T(8,128)(2,1)}, u32[]{:S(2)}, u32[]{:S(2)}) collective-permute-start(bf16[8,256,256]{2,1,0:T(8,128)(2,1)S(1)} %collective-permute-done.11.refs_4_), channel_id=1, source_target_pairs={{0,1},{1,0},{2,3},{3,2},{4,5},{5,4},{6,7},{7,6},{8,9},{9,8},{10,11... | collective-permute-start | bytes 3145736 | tf_op jit(solution)/shard_map/ppermute | solution.py:28
  129.9 44.6 %copy-start.6 = (f32[1024]{0:T(1024)S(1)}, f32[1024]{0:T(1024)}, u32[]{:S(2)}) copy-start(f32[1024]{0:T(1024)} %param.8) | copy-start | bytes 12292
  129.9 44.6 %copy-start.7 = (s32[16,8]{0,1:T(8,128)S(1)}, s32[16,8]{0,1:T(8,128)}, u32[]{:S(2)}) copy-start(s32[16,8]{0,1:T(8,128)} %param.9) | copy-start | bytes 1540
  142.3 57.8 %all-to-all-start.2 = ((bf16[16,384,256]{2,1,0:T(8,128)(2,1)}), bf16[16,384,256]{2,1,0:T(8,128)(2,1)}, u32[]{:S(2)}, u32[]{:S(2)}) async-start(bf16[16,384,256]{2,1,0:T(8,128)(2,1)} %slice.12), calls=%async_computation.2 | async-start | bytes 6291456 | tf_op jit(solution)/shard_map/all_to_all | solution.py:287
  147.5 25.8 %collective-permute-start.19 = (bf16[8,256,256]{2,1,0:T(8,128)(2,1)S(1)}, bf16[8,256,256]{2,1,0:T(8,128)(2,1)}, u32[]{:S(2)}, u32[]{:S(2)}) collective-permute-start(bf16[8,256,256]{2,1,0:T(8,128)(2,1)S(1)} %collective-permute-done.11.refs_4_), channel_id=1, source_target_pairs={{0,32},{32,64},{64,96},{96,0},{1,33},{33,65},{65,97},{97,1},{2,34}... | collective-permute-start | bytes 3145736 | tf_op jit(solution)/shard_map/ppermute | solution.py:17
  148.1 26.4 %collective-permute-start.21 = (bf16[8,256,256]{2,1,0:T(8,128)(2,1)}, bf16[8,256,256]{2,1,0:T(8,128)(2,1)}, u32[]{:S(2)}, u32[]{:S(2)}) collective-permute-start(bf16[8,256,256]{2,1,0:T(8,128)(2,1)} %collective-permute-done.17.refs_10_), channel_id=1, source_target_pairs={{0,96},{32,0},{64,32},{96,64},{1,97},{33,1},{65,33},{97,65},{2,98}... | collective-permute-start | bytes 3145736 | tf_op jit(solution)/shard_map/ppermute | solution.py:17
  150.3 25.1 %collective-permute-start.14 = (bf16[8,256,256]{2,1,0:T(8,128)(2,1)}, bf16[8,256,256]{2,1,0:T(8,128)(2,1)}, u32[]{:S(2)}, u32[]{:S(2)}) collective-permute-start(bf16[8,256,256]{2,1,0:T(8,128)(2,1)} %copy-done.5), channel_id=1, source_target_pairs={{0,1},{1,0},{2,3},{3,2},{4,5},{5,4},{6,7},{7,6},{8,9},{9,8},{10,11... | collective-permute-start | bytes 3145736 | tf_op jit(solution)/shard_map/ppermute | solution.py:28
  151.1 24.3 %collective-permute-start.18 = (bf16[8,256,256]{2,1,0:T(8,128)(2,1)}, bf16[8,256,256]{2,1,0:T(8,128)(2,1)}, u32[]{:S(2)}, u32[]{:S(2)}) collective-permute-start(bf16[8,256,256]{2,1,0:T(8,128)(2,1)} %collective-permute-done.17.refs_10_), channel_id=1, source_target_pairs={{0,1},{1,0},{2,3},{3,2},{4,5},{5,4},{6,7},{7,6},{8,9},{9,8},{10,11... | collective-permute-start | bytes 3145736 | tf_op jit(solution)/shard_map/ppermute | solution.py:28
  151.2 24.2 %collective-permute-start.16 = (bf16[8,256,256]{2,1,0:T(8,128)(2,1)}, bf16[8,256,256]{2,1,0:T(8,128)(2,1)}, u32[]{:S(2)}, u32[]{:S(2)}) collective-permute-start(bf16[8,256,256]{2,1,0:T(8,128)(2,1)} %collective-permute-done.15.refs_8_), channel_id=1, source_target_pairs={{0,1},{1,0},{2,3},{3,2},{4,5},{5,4},{6,7},{7,6},{8,9},{9,8},{10,11... | collective-permute-start | bytes 3145736 | tf_op jit(solution)/shard_map/ppermute | solution.py:28
  173.3 18.1 %collective-permute-start.20 = (bf16[8,256,256]{2,1,0:T(8,128)(2,1)}, bf16[8,256,256]{2,1,0:T(8,128)(2,1)}, u32[]{:S(2)}, u32[]{:S(2)}) collective-permute-start(bf16[8,256,256]{2,1,0:T(8,128)(2,1)} %collective-permute-done.19.refs_0_.refs_12_), channel_id=1, source_target_pairs={{0,1},{1,0},{2,3},{3,2},{4,5},{5,4},{6,7},{7,6},{8,9},{9,8},{10,11... | collective-permute-start | bytes 3145736 | tf_op jit(solution)/shard_map/ppermute | solution.py:28
  174.5 17.0 %collective-permute-start.22 = (bf16[8,256,256]{2,1,0:T(8,128)(2,1)}, bf16[8,256,256]{2,1,0:T(8,128)(2,1)}, u32[]{:S(2)}, u32[]{:S(2)}) collective-permute-start(bf16[8,256,256]{2,1,0:T(8,128)(2,1)} %collective-permute-done.21.refs_2_.refs_14_), channel_id=1, source_target_pairs={{0,1},{1,0},{2,3},{3,2},{4,5},{5,4},{6,7},{7,6},{8,9},{9,8},{10,11... | collective-permute-start | bytes 3145736 | tf_op jit(solution)/shard_map/ppermute | solution.py:28
